TPU v7x, 256 devices: a whole 4x4x8 slice. The times are simulated.
256 devices in a mesh: gz: 16 (over y, x), dom: 16 (over z, core).
Axes of the slice: x: 4, y: 4, z: 8, core: 2. Of those that a mesh axis runs over, the one named last changes fastest.
Arguments:
- volume: float32 [768, 4, 384], P('gz'), may hold values from -6 to 6
- observed: bfloat16 [4096, 4, 384], P(('gz', 'dom')), may hold values from -6 to 6
- ctf_table: float32 [32, 2, 384], replicated, may hold values from -1 to 1
- ctf_class: int32 [4096], P(('gz', 'dom')), may hold values from 0 to 31
- bin_ids: int32 [4096], P(('gz', 'dom')), may hold values from 0 to 127
Outputs:
- pose_score: float32 [4096], P(('gz', 'dom'))
- backprojection: float32 [768, 4, 384], P(('gz', 'dom'))
All inputs are finite; a program needn't handle non-finite values.
Results may differ from a plain program's by a relative error of at most 0.0034.
Values may be sent and summed in bfloat16 or wider, within the bound.
A program may use at most 64 MiB of HBM per device.

v0:
```python
import math

import jax
import jax.numpy as jnp
from jax import lax
from jax.sharding import PartitionSpec as P

NZ = 768
NB_DEV = 8
NCTF = 32
ITERS = 3


epsilon = 1e-05


def kernel(offset):
    inside = jnp.abs(offset) < 1.0
    falloff = 1.0 - offset * offset
    return (
        jnp.where(inside, falloff * falloff, 0.0),
        jnp.where(inside, -4.0 * offset * falloff, 0.0),
    )


def geometry(bin_index, planes, total_bins, samples, columns):
    tilt_angle = -0.5 * math.pi + math.pi * (bin_index.astype(jnp.float32) + 0.5) / total_bins
    sine_value = jnp.sin(tilt_angle)
    cosine = jnp.cos(tilt_angle)
    radius = jnp.arange(samples).astype(jnp.float32)
    centre = 0.5 * NZ + radius * sine_value
    z_value, z_slope = kernel(planes[None, :] - centre[:, None])
    z_slope = z_slope * (-radius * cosine / samples)[:, None]
    x_value, x_slope = kernel(
        jnp.arange(columns).astype(jnp.float32)[None, :] - (radius * cosine)[:, None]
    )
    x_slope = x_slope * (radius * sine_value / samples)[:, None]
    return (z_value, z_slope, jnp.concatenate([x_value, x_slope], 0))


def contrast_of(classes, ctf_table, count, stacked_rows, samples):
    class_onehot = (classes[:, None] == jnp.arange(NCTF, dtype=jnp.int32)[None, :]).astype(
        jnp.float32
    )
    contrast = jnp.dot(
        class_onehot,
        ctf_table.reshape(NCTF, -1),
        precision=lax.Precision.HIGHEST,
        preferred_element_type=jnp.float32,
    )
    contrast = contrast.reshape(count, stacked_rows // 2, samples)
    return jnp.concatenate([contrast, contrast], 1)


def local(volume, observed, ctf_table, ctf_class, bin_ids):
    depth_local = volume.shape[0]
    stacked_rows = volume.shape[1]
    columns = volume.shape[2]
    samples = observed.shape[2]
    particles = observed.shape[0]
    total_bins = NB_DEV * lax.axis_size("dom")
    first_bin = lax.axis_index("dom") * NB_DEV
    planes = (lax.axis_index("gz") * depth_local + jnp.arange(depth_local, dtype=jnp.int32)).astype(
        jnp.float32
    )
    flat_volume = volume.reshape(depth_local * stacked_rows, columns)

    def extract(offset):
        z_value, z_slope, x_weights = geometry(
            first_bin + offset, planes, total_bins, samples, columns
        )
        resampled = jnp.dot(
            flat_volume,
            x_weights.T,
            precision=lax.Precision.HIGHEST,
            preferred_element_type=jnp.float32,
        )
        resampled = resampled.reshape(depth_local, stacked_rows, 2 * samples)
        direct = resampled[:, :, :samples]
        tilted = resampled[:, :, samples:]
        leading = jnp.sum(direct * z_value.T[:, None, :], axis=0)
        second = jnp.sum(direct * z_slope.T[:, None, :] + tilted * z_value.T[:, None, :], axis=0)
        return jnp.concatenate([leading, second], 0)

    partial_slices = lax.map(extract, jnp.arange(NB_DEV, dtype=jnp.int32))
    reduced = lax.psum(partial_slices, "gz")
    gathered = lax.all_gather(reduced.astype(jnp.bfloat16), "dom", axis=0, tiled=True)
    bin_onehot = bin_ids[:, None] == jnp.arange(total_bins, dtype=jnp.int32)[None, :]
    picked = jnp.dot(
        bin_onehot.astype(jnp.bfloat16),
        gathered.reshape(total_bins, -1),
        preferred_element_type=jnp.float32,
    )
    picked = picked.reshape(particles, 2 * stacked_rows, samples)
    contrast = contrast_of(ctf_class, ctf_table, particles, stacked_rows, samples)
    measured = observed.astype(jnp.float32)
    predicted = contrast * picked[:, :stacked_rows]
    tangent = contrast * picked[:, stacked_rows:]
    curvature = jnp.sum(tangent * tangent, axis=(1, 2)) + epsilon
    shift = jnp.zeros((particles,), jnp.float32)
    for iteration in range(ITERS):
        residual_map = measured - predicted - shift[:, None, None] * tangent
        shift = shift + 0.5 * jnp.sum(residual_map * tangent, axis=(1, 2)) / curvature
    pose_score = shift * jnp.sqrt(curvature)
    onehot_float = bin_onehot.astype(jnp.float32)
    weighted = contrast * measured
    contributions = jnp.concatenate([weighted, shift[:, None, None] * weighted], 1).reshape(
        particles, -1
    )
    totals = jnp.dot(
        onehot_float.T,
        contributions,
        precision=lax.Precision.HIGHEST,
        preferred_element_type=jnp.float32,
    )
    totals = lax.psum(totals, ("gz", "dom"))
    owned = lax.dynamic_slice_in_dim(totals, first_bin, NB_DEV, 0)
    owned = owned.reshape(NB_DEV, 2 * stacked_rows, samples)

    def spread_back(offset, accumulated):
        z_value, z_slope, x_weights = geometry(
            first_bin + offset, planes, total_bins, samples, columns
        )
        summed = lax.dynamic_index_in_dim(owned, offset, 0, keepdims=False)
        direct = summed[:stacked_rows]
        tilted = summed[stacked_rows:]
        z_plain = z_value.T[:, None, :]
        z_tilted = z_slope.T[:, None, :]
        leading = z_plain * direct[None] + z_tilted * tilted[None]
        second = z_plain * tilted[None]
        stacked = jnp.concatenate([leading, second], 2).reshape(
            depth_local * stacked_rows, 2 * samples
        )
        return accumulated + jnp.dot(
            stacked, x_weights, precision=lax.Precision.HIGHEST, preferred_element_type=jnp.float32
        )

    backprojected = lax.fori_loop(
        0, NB_DEV, spread_back, jnp.zeros((depth_local * stacked_rows, columns), jnp.float32)
    )
    backprojected = backprojected.reshape(depth_local, stacked_rows, columns)
    plane_share = lax.psum_scatter(backprojected, "dom", scatter_dimension=0, tiled=True)
    return (pose_score, plane_share)


def solution(mesh):
    return jax.shard_map(
        local,
        mesh=mesh,
        in_specs=(
            P("gz", None, None),
            P(("gz", "dom"), None, None),
            P(),
            P(("gz", "dom")),
            P(("gz", "dom")),
        ),
        out_specs=(P(("gz", "dom")), P(("gz", "dom"), None, None)),
        check_vma=False,
    )
```

profile of v0, /device:TPU:1, one launch (start us, length us, event | category | flops | bytes accessed | tf_op | source)
XLA Modules:
  0.0 525.4 jit_solution(10506065352268123500)
XLA Ops:
  7.2 1.1 reshape.295
  8.3 28.8 %while.29 = (s32[]{:T(128)}, f32[8,8,384]{2,1,0:T(8,128)S(1)}, s32[8]{0:T(128)S(1)}, s32[]{:T(128)}, f32[192,384]{1,0:T(8,128)S(1)}, /*index=5*/s32[]{:T(128)}, s32[]{:T(128)}, f32[]{:T(128)}, f32[]{:T(128)}, f32[]{:T(128)}) while((s32[]{:T(128)}, f32[8,8,384]{2,1,0:T(8,128)S(1)}, s32[8]{0:T(128)S(1)}, s32[]{:T(128)}, ...), condition=%wide.region_3.4_spmd.clone, body=%wide.region_0.3_spmd.clone.sunk | while | flops 682043264 | bytes 5361225 | solution.py:85
  8.3 0.6 dynamic_slice.26
  10.0 1.4 convolution_bitcast_fusion.2
  11.9 0.6 dynamic_slice.26
  13.5 1.5 convolution_bitcast_fusion.2
  15.5 0.6 dynamic_slice.26
  17.2 1.4 convolution_bitcast_fusion.2
  20.7 1.5 convolution_bitcast_fusion.2
  24.4 1.4 convolution_bitcast_fusion.2
  28.0 1.5 convolution_bitcast_fusion.2
  31.6 1.4 convolution_bitcast_fusion.2
  35.2 1.5 convolution_bitcast_fusion.2
  37.2 62.0 %psum.14 = bf16[8,8,384]{2,1,0:T(8,128)(2,1)S(1)} all-reduce(f32[8,8,384]{2,1,0:T(8,128)S(1)} %get-tuple-element.211), channel_id=1, replica_groups=mesh['gz'=16,'dom'=16] {'gz'}, use_global_device_ids=true, to_apply=%region_4.5 | all-reduce | flops 24576 | bytes 147456 | tf_op jit(solution)/shard_map/psum | solution.py:86
  99.1 36.8 %all_gather.3 = bf16[128,8,384]{2,1,0:T(8,128)(2,1)S(1)} all-gather(bf16[8,8,384]{2,1,0:T(8,128)(2,1)S(1)} %psum.14), channel_id=1, replica_groups=mesh['gz'=16,'dom'=16] {'dom'}, dimensions={0}, use_global_device_ids=true | all-gather | bytes 835584 | tf_op jit(solution)/shard_map/all_gather | solution.py:87
  136.0 0.6 copy.17
  138.4 2.0 fusion.63
  140.5 251.3 %all-reduce.4.cloned.1.call-done = f32[128,3072]{1,0:T(8,128)} async-done(((f32[128,3072]{1,0:T(8,128)}), f32[128,3072]{1,0:T(8,128)}) %all-reduce.4.cloned.1.call-update) | async-done | bytes 1572880 | tf_op jit(solution)/shard_map/psum | solution.py:116
  391.8 0.9 constant_dynamic-slice_fusion.1
  392.7 17.9 %while.30 = (s32[]{:T(128)}, f32[192,384]{1,0:T(8,128)S(1)}, s32[]{:T(128)}, f32[8,8,384]{2,1,0:T(8,128)S(1)}, s32[]{:T(128)}, /*index=5*/s32[]{:T(128)}, f32[]{...) while((s32[]{:T(128)}, f32[192,384]{1,0:T(8,128)S(1)}, s32[]{:T(128)}, ...), condition=%wide.region_11.12_spmd.clone, body=%wide.region_10.11_spmd.clone.sunk | while | flops 682190720 | bytes 5656159 | solution.py:138
  393.7 1.2 fusion.96
  395.9 1.2 fusion.96
  398.2 1.2 fusion.96
  400.4 1.2 fusion.96
  402.6 1.2 fusion.96
  404.9 1.2 fusion.96
  407.1 1.2 fusion.96
  409.4 1.2 fusion.96
  410.6 0.8 reshape.299
  411.4 0.6 dynamic-slice
  412.7 104.5 %all-reduce.6.cloned.1.call-done = f32[48,4,384]{2,1,0:T(4,128)} async-done(((f32[48,4,384]{2,1,0:T(4,128)}), f32[48,4,384]{2,1,0:T(4,128)}) %all-reduce.6.cloned.1.call-update) | async-done | bytes 294928
  517.2 1.3 constant_dynamic-slice_fusion
  (186 shorter events, 16.8 us)
Async XLA Ops:
  7.2 384.6 %all-reduce.4.cloned.1.call-start = ((), (), s32[]{:S(2)}) async-start(), calls=%async_computation | async-start | bytes 3145728 | tf_op jit(solution)/shard_map/psum | solution.py:116
  99.1 37.5 %copy-start.2 = (s32[16]{0:T(128)S(1)}, s32[16]{0:T(128)}, u32[]{:S(2)}) copy-start(s32[16]{0:T(128)} %param.13) | copy-start | bytes 196
  136.0 0.9 copy-start.1
  136.0 1.0 copy-start.3
  136.0 1.2 copy-start
  140.4 376.8 %all-reduce.6.cloned.1.call-start = ((), (), s32[]{:S(2)}) async-start(), calls=%async_computation.1 | async-start | bytes 589824
  392.7 18.7 %copy-start.4 = (u32[256]{0:T(256)S(1)}, u32[256]{0:T(256)}, u32[]{:S(2)}) copy-start(u32[256]{0:T(256)} %constant.211) | copy-start | bytes 3076
Sparse Core Ops, SparseCore 0:
  140.6 251.1 all-reduce.3
  411.6 105.6 all-reduce.5
where the time goes:
time: 526 us; the launch traced here: 525 us
  waiting for transfers between devices  356 us (68%)
  blocking collectives  98.8 us (19%)
  matrix products  24.2 us (5%)
  between operations  14.8 us (3%)
  local copies, waits for them, and re-layouts  13.1 us (2%)
  other arithmetic  10.1 us (2%)
  loops' own time  8.51 us (2%)
    psum x1, waiting for transfers between devices, local(): totals = lax.psum(totals, ('gz', 'dom'))  251 us
    unnamed x3, waiting for transfers between devices  105 us
    psum x1, blocking collectives, local(): reduced = lax.psum(partial_slices, 'gz')  62 us
    all_gather x1, blocking collectives, local(): lax.all_gather(reduced.astype(jnp.bfloat16), 'dom', axis=0, tiled=True)  36.8 us
    dot_general x8, matrix products, extract(): jnp.dot(flat_volume, x_weights.T, precision=lax.Precision.HIGHEST, prefer...  11.7 us
  transfers between devices with their start and end apart: 2, of which 2 were waited for; matrix products, arithmetic and copies ran while one was open for 0% of the time, Pallas kernels for 0%

commit v1 on v0

v1 whole, which is shorter than its diff:
```python
import math

import jax
import jax.numpy as jnp
from jax import lax
from jax.experimental import pallas as pl
from jax.experimental.pallas import tpu as pltpu
from jax.sharding import PartitionSpec as P

NZ = 768
NB = 128
NB_DEV = 8
NCTF = 32
ITERS = 3
EPS = 1e-05
G = 16
D = 16
SLAB = 48
R = 4
X = 384
U = 384
PART = 16
ALLP = PART * D
WC = R * U
EXT = 128
NCH = 12
F32 = jnp.float32
BF16 = jnp.bfloat16
NT = (((1,), (1,)), ((), ()))


def iota(shape, dim):
    return lax.broadcasted_iota(jnp.int32, shape, dim)


def gz_copy(src, dst, send, recv, to):
    return pltpu.make_async_remote_copy(
        src_ref=src, dst_ref=dst, send_sem=send, recv_sem=recv,
        device_id={"gz": to}, device_id_type=pl.DeviceIdType.MESH)


def dom_copy(src, dst, send, recv, to):
    return pltpu.make_async_remote_copy(
        src_ref=src, dst_ref=dst, send_sem=send, recv_sem=recv,
        device_id={"dom": to}, device_id_type=pl.DeviceIdType.MESH)


def body(vol, obs, ctf, cls, bins, pose_out, back_out,
         vb, kt, kl, kz, kzd, sc, sp, sp_in, s_all, ss, ss_in, t_all, t32,
         w_all, c2h, c2l, ls, acc, bk, bk_in, pose_s, pose_in,
         w_send, w_recv, f_send, f_recv,
         rs_send, rs_recv, ag_send, ag_recv,
         rs2_send, rs2_recv, ag2_send, ag2_recv,
         b_send, b_recv, p_send, p_recv):
    g = lax.axis_index("gz")
    d = lax.axis_index("dom")
    core = lax.rem(d, 2)
    zpos = lax.div(d, 2)
    sib = d + 1 - 2 * core
    first_bin = d * NB_DEV

    barrier = pltpu.get_barrier_semaphore()
    for i in range(1, G):
        pl.semaphore_signal(barrier, inc=1, device_id={"gz": lax.rem(g + i, G)},
                            device_id_type=pl.DeviceIdType.MESH)
    for i in range(1, D):
        pl.semaphore_signal(barrier, inc=1, device_id={"dom": lax.rem(d + i, D)},
                            device_id_type=pl.DeviceIdType.MESH)

    rows = iota((PART, EXT), 0)
    lanes = iota((PART, EXT), 1)
    cls_col = jnp.zeros((PART, EXT), jnp.int32)
    bin_col = jnp.zeros((PART, EXT), jnp.int32)
    for i in range(PART):
        cls_col = jnp.where(rows == i, cls[i], cls_col)
        bin_col = jnp.where(rows == i, bins[i], bin_col)
    cls_hot = (cls_col == lanes).astype(F32)
    table = jnp.concatenate([ctf[:, 0, :], ctf[:, 1, :]], 1)
    contrast = jnp.dot(cls_hot[:, :NCTF], table, precision=lax.Precision.HIGHEST,
                       preferred_element_type=F32)
    for r in range(R):
        y = r % 2
        image = obs[:, r, :].astype(F32)
        w_all[d, :, r * U:(r + 1) * U] = (image * contrast[:, y * U:(y + 1) * U]).astype(BF16)
    extra = jnp.where(lanes == NCTF, bin_col.astype(F32), cls_hot)
    w_all[d, :, WC:] = extra.astype(BF16)

    pl.semaphore_wait(barrier, (G - 1) + (D - 1))

    for i in range(1, D // 2):
        to = lax.rem(zpos + i, D // 2) * 2 + core
        dom_copy(w_all.at[d], w_all.at[d], w_send.at[i], w_recv.at[d], to).start()
    dom_copy(w_all.at[d], w_all.at[d], f_send.at[0], f_recv.at[d], sib).start()

    square = table * table
    high = square.astype(BF16)
    c2h[...] = jnp.zeros_like(c2h)
    c2l[...] = jnp.zeros_like(c2l)
    c2h[:NCTF, :] = high
    c2l[:NCTF, :] = (square - high.astype(F32)).astype(BF16)

    for r in range(R):
        plane_rows = vol[:, r, :]
        coarse = plane_rows.astype(BF16)
        vb[r * SLAB:(r + 1) * SLAB, :] = coarse
        vb[(R + r) * SLAB:(R + r + 1) * SLAB, :] = (plane_rows - coarse.astype(F32)).astype(BF16)
    bin_index = (first_bin + iota((NB_DEV, 128), 0)).astype(F32)
    theta = -0.5 * math.pi + math.pi * (bin_index + 0.5) / NB
    sc[:NB_DEV, :] = jnp.sin(theta)
    sc[NB_DEV:, :] = jnp.cos(theta)
    radius = iota((1, U), 1).astype(F32)
    plane = (g * SLAB + iota((SLAB, U), 0)).astype(F32)
    column = iota((X, U), 0).astype(F32)

    def extract(b, carry):
        sine = jnp.concatenate([sc[pl.ds(b, 1), :]] * 3, 1)
        cosine = jnp.concatenate([sc[pl.ds(NB_DEV + b, 1), :]] * 3, 1)
        tx = column - radius * cosine
        fx = jnp.maximum(1.0 - tx * tx, 0.0)
        kx = fx * fx
        kxd = (tx * fx) * (radius * sine * (-4.0 / U))
        kx_high = kx.astype(BF16)
        kxd_high = kxd.astype(BF16)
        kt[b, :, :U] = kx_high
        kt[b, :, U:] = kxd_high
        kl[:, :U] = (kx - kx_high.astype(F32)).astype(BF16)
        kl[:, U:] = (kxd - kxd_high.astype(F32)).astype(BF16)
        tz = plane - (0.5 * NZ + radius * sine)
        fz = jnp.maximum(1.0 - tz * tz, 0.0)
        wz = fz * fz
        wd = (tz * fz) * (radius * cosine * (4.0 / U))
        kz[b] = wz
        kzd[b] = wd
        stacked = jnp.dot(vb[...], kt[b], preferred_element_type=F32)
        both = stacked[:R * SLAB] + stacked[R * SLAB:] + jnp.dot(
            vb[:R * SLAB, :], kl[...], preferred_element_type=F32)
        for r in range(R):
            direct = both[r * SLAB:(r + 1) * SLAB, :U]
            tilted = both[r * SLAB:(r + 1) * SLAB, U:]
            lead = jnp.sum(direct * wz, axis=0, keepdims=True)
            second = jnp.sum(direct * wd + tilted * wz, axis=0, keepdims=True)
            for j in range(3):
                at = pl.ds((r % 2) * 8 + b, 1)
                sp[3 * (r // 2) + j, at, :] = lead[:, 128 * j:128 * (j + 1)]
                sp[3 * (2 + r // 2) + j, at, :] = second[:, 128 * j:128 * (j + 1)]
        return carry

    lax.fori_loop(0, NB_DEV, extract, 0)

    offset = 4 * core
    mine = lax.rem(g - offset + G, G)
    reduces = mine < NCH

    def sum_start(src, src_in, send, recv):
        for i in range(1, G):
            to = lax.rem(g + i, G)
            q = lax.rem(to - offset + G, G)

            @pl.when(q < NCH)
            def _():
                gz_copy(src.at[q], src_in.at[g], send.at[i], recv.at[g], to).start()

    def sum_reduce(src, src_in, out, recv, send2, recv2):
        @pl.when(reduces)
        def _():
            src_in[g] = src[mine]
            for i in range(1, G):
                frm = lax.rem(g + i, G)
                gz_copy(src.at[0], src_in.at[frm], recv.at[frm], recv.at[frm], frm).wait_recv()
            total = src_in[0]
            for i in range(1, G):
                total = total + src_in[i]
            out[mine] = total.astype(out.dtype)
            for i in range(1, G):
                to = lax.rem(g + i, G)
                gz_copy(out.at[mine], out.at[mine], send2.at[i], recv2.at[mine], to).start()

    def sum_wait(out, recv2):
        for q in range(NCH):
            @pl.when(mine != q)
            def _():
                gz_copy(out.at[q], out.at[q], recv2.at[q], recv2.at[q], lax.rem(g + 1, G)).wait_recv()

    def sum_finish(src, src_in, out, send, recv, send2):
        for i in range(1, G):
            to = lax.rem(g + i, G)
            q = lax.rem(to - offset + G, G)

            @pl.when(q < NCH)
            def _():
                gz_copy(src.at[q], src_in.at[g], send.at[i], recv.at[g], to).wait_send()

            @pl.when(reduces)
            def _():
                gz_copy(out.at[0], out.at[0], send2.at[i], send2.at[i], to).wait_send()

    sum_start(sp, sp_in, rs_send, rs_recv)
    sum_reduce(sp, sp_in, s_all, rs_recv, ag_send, ag_recv)

    for i in range(1, D // 2):
        frm = lax.rem(zpos + i, D // 2) * 2 + core
        dom_copy(w_all.at[frm], w_all.at[frm], w_recv.at[frm], w_recv.at[frm], sib).wait_recv()
        dom_copy(w_all.at[frm], w_all.at[frm], f_send.at[i], f_recv.at[frm], sib).start()

    sum_wait(s_all, ag_recv)

    def rows_of(kind, r):
        k = 2 * kind + r // 2
        half = (r % 2) * 8
        return jnp.concatenate(
            [s_all[3 * k + j].astype(F32)[half:half + 8, :] for j in range(3)], 1)

    lead = [rows_of(0, r) for r in range(R)]
    slope = [rows_of(1, r) for r in range(R)]
    curve = jnp.concatenate([slope[y] * slope[y] + slope[y + 2] * slope[y + 2] for y in range(2)], 1)
    cross = jnp.concatenate([lead[y] * slope[y] + lead[y + 2] * slope[y + 2] for y in range(2)], 1)
    quad = jnp.concatenate([curve, cross], 0)
    quad_high = quad.astype(BF16)
    quad_low = (quad - quad_high.astype(F32)).astype(BF16)
    first = lax.dot_general(jnp.concatenate([quad_high, quad_low], 0), c2h[...], NT,
                            preferred_element_type=F32)
    tables = first[:16] + first[16:] + lax.dot_general(quad_high, c2l[...], NT,
                                                       preferred_element_type=F32)
    tables_high = tables.astype(BF16)
    tables_low = (tables - tables_high.astype(F32)).astype(BF16)
    pick = (iota((8, EXT), 1) == NCTF).astype(F32).astype(BF16)
    zero = jnp.zeros((8, EXT), BF16)
    lookup = jnp.concatenate([tables_high, tables_low, pick, zero], 0)
    slope_rows = jnp.concatenate(slope, 1).astype(BF16)

    for i in range(0, D // 2):
        frm = lax.rem(zpos + i, D // 2) * 2 + 1 - core
        dom_copy(w_all.at[frm], w_all.at[frm], f_recv.at[frm], f_recv.at[frm], sib).wait_recv()

    images = w_all[:, :, :WC].reshape(ALLP, WC)
    marks = w_all[:, :, WC:].reshape(ALLP, EXT)
    looked = lax.dot_general(lookup, marks, NT, preferred_element_type=F32)
    along = lax.dot_general(slope_rows, images, NT, preferred_element_type=F32)
    held = looked[0:8] + looked[16:24]
    crossed = looked[8:16] + looked[24:32]
    own = (first_bin + iota((8, ALLP), 0)).astype(F32) == looked[32:40]
    mask = own.astype(F32)
    power = jnp.sum(mask * held, axis=0, keepdims=True)
    match = jnp.sum(mask * (along - crossed), axis=0, keepdims=True)
    curvature = power + EPS
    shift = jnp.zeros_like(power)
    for _ in range(ITERS):
        shift = shift + 0.5 * (match - shift * power) / curvature
    pose_s[...] = shift * jnp.sqrt(curvature)
    moved = mask * shift
    moved_high = moved.astype(BF16)
    moved_low = (moved - moved_high.astype(F32)).astype(BF16)
    spread = jnp.concatenate([mask.astype(BF16), moved_high, moved_low, jnp.zeros((8, ALLP), BF16)], 0)
    sums = jnp.dot(spread, images, preferred_element_type=F32)
    for q in range(NCH):
        part = sums[:, 128 * q:128 * (q + 1)]
        ss[q] = jnp.concatenate([part[:8], part[8:16] + part[16:24]], 0)

    sum_start(ss, ss_in, rs2_send, rs2_recv)
    for i in range(1, D):
        to = lax.rem(d + i, D)
        dom_copy(pose_s, pose_in.at[d], p_send.at[i], p_recv.at[d], to).start()
    sum_reduce(ss, ss_in, t_all, rs2_recv, ag2_send, ag2_recv)
    sum_wait(t_all, ag2_recv)

    for q in range(NCH):
        t32[:, 128 * q:128 * (q + 1)] = t_all[q]
    acc[...] = jnp.zeros_like(acc)

    def spread_back(b, carry):
        wz = kz[b]
        wd = kzd[b]
        for r in range(R):
            plain = t32[pl.ds(b, 1), r * U:(r + 1) * U]
            sloped = t32[pl.ds(8 + b, 1), r * U:(r + 1) * U]
            ls[r * SLAB:(r + 1) * SLAB, :U] = (wz * plain + wd * sloped).astype(BF16)
            ls[r * SLAB:(r + 1) * SLAB, U:] = (wz * sloped).astype(BF16)
        acc[...] += lax.dot_general(ls[...], kt[b], NT, preferred_element_type=F32)
        return carry

    lax.fori_loop(0, NB_DEV, spread_back, 0)

    row = iota((256, R * SLAB), 0)
    within = lax.rem(row, 16)
    source = lax.rem(row, 4) * SLAB + 3 * lax.div(row, 16) + lax.div(within, 4)
    order = ((iota((256, R * SLAB), 1) == source) & (within < 12)).astype(F32).astype(BF16)
    ordered = jnp.dot(order, acc[...].astype(BF16), preferred_element_type=F32)
    bk[...] = ordered.astype(BF16).reshape(D, 16, X)
    for i in range(1, D):
        to = lax.rem(d + i, D)
        dom_copy(bk.at[to], bk_in.at[d], b_send.at[i], b_recv.at[d], to).start()

    pose_in[d] = pose_s[...]
    for i in range(1, D):
        frm = lax.rem(d + i, D)
        dom_copy(pose_s, pose_in.at[frm], p_recv.at[frm], p_recv.at[frm], frm).wait_recv()
    pose = pose_in[0]
    for i in range(1, D):
        pose = pose + pose_in[i]
    lane = iota((8, ALLP), 1)
    kept = jnp.where(lax.div(lane, PART) == d, pose, 0.0)
    choose = (lax.rem(iota((ALLP, 128), 0), PART) == iota((ALLP, 128), 1)).astype(F32)
    picked = jnp.dot(kept, choose, precision=lax.Precision.HIGHEST, preferred_element_type=F32)
    pose_out[...] = picked[0:1, :PART]

    bk_in[d] = bk[d]
    for i in range(1, D):
        frm = lax.rem(d + i, D)
        dom_copy(bk.at[0], bk_in.at[frm], b_recv.at[frm], b_recv.at[frm], frm).wait_recv()
    total = bk_in[0].astype(F32)
    for i in range(1, D):
        total = total + bk_in[i].astype(F32)
    for k in range(3):
        back_out[k] = total[4 * k:4 * k + 4]

    sum_finish(sp, sp_in, s_all, rs_send, rs_recv, ag_send)
    sum_finish(ss, ss_in, t_all, rs2_send, rs2_recv, ag2_send)
    for i in range(1, D // 2):
        dom_copy(w_all.at[d], w_all.at[d], w_send.at[i], w_send.at[i], sib).wait_send()
    for i in range(0, D // 2):
        dom_copy(w_all.at[d], w_all.at[d], f_send.at[i], f_send.at[i], sib).wait_send()
    for i in range(1, D):
        dom_copy(bk.at[0], bk_in.at[d], b_send.at[i], b_send.at[i], sib).wait_send()
        dom_copy(pose_s, pose_in.at[d], p_send.at[i], p_send.at[i], sib).wait_send()


def local(volume, observed, ctf_table, ctf_class, bin_ids):
    vmem = pl.BlockSpec(memory_space=pltpu.VMEM)
    smem = pl.BlockSpec(memory_space=pltpu.SMEM)
    dma = pltpu.SemaphoreType.DMA
    pose, back = pl.pallas_call(
        body,
        out_shape=(jax.ShapeDtypeStruct((1, PART), F32), jax.ShapeDtypeStruct((3, R, X), F32)),
        in_specs=[vmem, vmem, vmem, smem, smem],
        out_specs=(vmem, vmem),
        scratch_shapes=[
            pltpu.VMEM((2 * R * SLAB, X), BF16),
            pltpu.VMEM((NB_DEV, X, 2 * U), BF16),
            pltpu.VMEM((X, 2 * U), BF16),
            pltpu.VMEM((NB_DEV, SLAB, U), F32),
            pltpu.VMEM((NB_DEV, SLAB, U), F32),
            pltpu.VMEM((2 * NB_DEV, 128), F32),
            pltpu.VMEM((NCH, 16, 128), F32),
            pltpu.VMEM((G, 16, 128), F32),
            pltpu.VMEM((NCH, 16, 128), BF16),
            pltpu.VMEM((NCH, 16, 128), F32),
            pltpu.VMEM((G, 16, 128), F32),
            pltpu.VMEM((NCH, 16, 128), F32),
            pltpu.VMEM((16, WC), F32),
            pltpu.VMEM((D, PART, WC + EXT), BF16),
            pltpu.VMEM((EXT, 2 * U), BF16),
            pltpu.VMEM((EXT, 2 * U), BF16),
            pltpu.VMEM((R * SLAB, 2 * U), BF16),
            pltpu.VMEM((R * SLAB, X), F32),
            pltpu.VMEM((D, 16, X), BF16),
            pltpu.VMEM((D, 16, X), BF16),
            pltpu.VMEM((1, ALLP), F32),
            pltpu.VMEM((D, 1, ALLP), F32),
        ] + [dma((16,))] * 16,
        compiler_params=pltpu.CompilerParams(
            collective_id=0, has_side_effects=True, vmem_limit_bytes=32 << 20),
        name="tilt_refine",
    )(volume, observed, ctf_table, ctf_class, bin_ids)
    return (pose.reshape(PART), back)


def solution(mesh):
    return jax.shard_map(
        local,
        mesh=mesh,
        in_specs=(
            P("gz", None, None),
            P(("gz", "dom"), None, None),
            P(),
            P(("gz", "dom")),
            P(("gz", "dom")),
        ),
        out_specs=(P(("gz", "dom")), P(("gz", "dom"), None, None)),
        check_vma=False,
    )
```

time: 526 us -> 57.6 us (0.11)
  waiting for transfers between devices: 356 us -> 0 us
  blocking collectives: 98.8 us -> 0 us
  Pallas kernels: 0 us -> 51.7 us
  matrix products: 24.2 us -> 0 us
  between operations: 14.8 us -> 0.65 us
  other arithmetic: 10.1 us -> 0 us
  loops' own time: 8.51 us -> 0 us
  local copies, waits for them, and re-layouts: 13.1 us -> 5.07 us
    psum x1 -> x0, waiting for transfers between devices: 251 us -> none  [local(): totals = lax.psum(totals, ('gz', 'dom'))]
    unnamed x3 -> x0, waiting for transfers between devices: 105 us -> none
    psum x1 -> x0, blocking collectives: 62 us -> none  [local(): reduced = lax.psum(partial_slices, 'gz')]
    pallas_call x0 -> x1, Pallas kernels: none -> 51.7 us  [local(): pl.pallas_call(body, out_shape=(jax.ShapeDtypeStruct((1, PART), F32), jax...]
    all_gather x1 -> x0, blocking collectives: 36.8 us -> none  [local(): lax.all_gather(reduced.astype(jnp.bfloat16), 'dom', axis=0, tiled=True)]
    dot_general x19 -> x0, matrix products: 24.2 us -> none  [the longest x8 11.7 us: extract(): jnp.dot(flat_volume, x_weights.T, precision=lax.Precision.HIGHEST, prefer...]
    another operation x2 -> x0, loops' own time: 8.51 us -> none  [the longest x1 6.42 us: local(): partial_slices = lax.map(extract, jnp.arange(NB_DEV, dtype=jnp.int32))]
    dynamic_slice x9 -> x0, local copies, waits for them, and re-layouts: 5.53 us -> none  [the longest x8 4.64 us: local(): partial_slices = lax.map(extract, jnp.arange(NB_DEV, dtype=jnp.int32))]
  transfers between devices with their start and end apart: 2 -> 0, of which waited for: 2 -> 0; matrix products, arithmetic and copies ran while one was open for 0% -> 0% of each run, Pallas kernels for 0% -> 0%
where the time goes in v1:
time: 57.6 us; the launch traced here: 57.4 us
  Pallas kernels  51.7 us (90%)
  local copies, waits for them, and re-layouts  5.07 us (9%)
  between operations  0.65 us (1%)
    pallas_call x1, Pallas kernels, local(): pl.pallas_call(body, out_shape=(jax.ShapeDtypeStruct((1, PART), F32), jax...  51.7 us
    unnamed x12, local copies, waits for them, and re-layouts  5.07 us

profile of v1, /device:TPU:1, one launch (start us, length us, event | category | flops | bytes accessed | tf_op | source)
XLA Modules:
  0.0 57.4 jit_solution(6203433232899361460)
XLA Ops:
  0.6 0.0 copy-start
  0.6 1.0 %copy-done = f32[48,4,384]{2,1,0:T(4,128)S(1)} copy-done((f32[48,4,384]{2,1,0:T(4,128)S(1)}, f32[48,4,384]{2,1,0:T(4,128)}, u32[]{:S(2)}) %copy-start) | copy-done | bytes 294936
  1.6 0.0 copy-start.1
  1.6 0.9 %copy-done.1 = f32[32,2,384]{2,1,0:T(2,128)S(1)} copy-done((f32[32,2,384]{2,1,0:T(2,128)S(1)}, f32[32,2,384]{2,1,0:T(2,128)}, u32[]{:S(2)}) %copy-start.1) | copy-done | bytes 98328
  2.5 0.0 copy-start.2
  2.5 0.8 %copy-done.2 = bf16[16,4,384]{2,1,0:T(4,128)(2,1)S(1)} copy-done((bf16[16,4,384]{2,1,0:T(4,128)(2,1)S(1)}, bf16[16,4,384]{2,1,0:T(4,128)(2,1)}, u32[]{:S(2)}) %copy-start.2) | copy-done | bytes 49176
  3.3 0.0 copy-start.3
  3.3 0.7 %copy-done.3 = s32[16]{0:T(128)S(1)} copy-done((s32[16]{0:T(128)S(1)}, s32[16]{0:T(128)}, u32[]{:S(2)}) %copy-start.3) | copy-done | bytes 88
  3.9 0.0 copy-start.4
  3.9 0.7 %copy-done.4 = s32[16]{0:T(128)S(1)} copy-done((s32[16]{0:T(128)S(1)}, s32[16]{0:T(128)}, u32[]{:S(2)}) %copy-start.4) | copy-done | bytes 88
  4.6 51.7 %tilt_refine.1 = (f32[1,16]{1,0:T(1,128)S(1)}, f32[3,4,384]{2,1,0:T(4,128)S(1)}) custom-call(f32[48,4,384]{2,1,0:T(4,128)S(1)} %copy-done, bf16[16,4,384]{2,1,0:T(4,128)(2,1)S(1)} %copy-done.2, f32[32,2,384]{2,1,0:T(2,128)S(1)} %copy-done.1, s32[16]{0:T(128)S(1)} %copy-done.3, s32[16]{0:T(128)S(1)} %copy-done.4), custom_call_target="tpu_custom_call" | custom-call | tf_op jit(solution)/shard_map/tilt_refine/pallas_call | solution.py:331
  56.3 0.5 copy.9
  56.8 0.6 %copy.10 = f32[3,4,384]{2,1,0:T(4,128)} copy(f32[3,4,384]{2,1,0:T(4,128)S(1)} %get-tuple-element.9) | data formatting | bytes 36864
Async XLA Ops:
  0.6 1.0 %copy-start = (f32[48,4,384]{2,1,0:T(4,128)S(1)}, f32[48,4,384]{2,1,0:T(4,128)}, u32[]{:S(2)}) copy-start(f32[48,4,384]{2,1,0:T(4,128)} %vol.1) | copy-start | bytes 884740
  1.6 0.9 %copy-start.1 = (f32[32,2,384]{2,1,0:T(2,128)S(1)}, f32[32,2,384]{2,1,0:T(2,128)}, u32[]{:S(2)}) copy-start(f32[32,2,384]{2,1,0:T(2,128)} %ctf.1) | copy-start | bytes 294916
  2.5 0.8 %copy-start.2 = (bf16[16,4,384]{2,1,0:T(4,128)(2,1)S(1)}, bf16[16,4,384]{2,1,0:T(4,128)(2,1)}, u32[]{:S(2)}) copy-start(bf16[16,4,384]{2,1,0:T(4,128)(2,1)} %obs.1) | copy-start | bytes 147460
  3.3 0.7 %copy-start.3 = (s32[16]{0:T(128)S(1)}, s32[16]{0:T(128)}, u32[]{:S(2)}) copy-start(s32[16]{0:T(128)} %cls.1) | copy-start | bytes 196
  3.9 0.7 %copy-start.4 = (s32[16]{0:T(128)S(1)}, s32[16]{0:T(128)}, u32[]{:S(2)}) copy-start(s32[16]{0:T(128)} %bins.1) | copy-start | bytes 196

commit v2 on v1

--- a/solution.py
+++ b/solution.py
@@ -45,8 +45,8 @@
         device_id={"dom": to}, device_id_type=pl.DeviceIdType.MESH)
 
 
-def body(vol, obs, ctf, cls, bins, pose_out, back_out,
-         vb, kt, kl, kz, kzd, sc, sp, sp_in, s_all, ss, ss_in, t_all, t32,
+def body(vol_hbm, obs_hbm, ctf_hbm, cls_hbm, bins_hbm, pose_out, back_out,
+         vol, obs, ctf, cls, bins, in_sem, vb, kt, kl, kz, kzd, sc, sp, sp_in, s_all, ss, ss_in, t_all, t32,
          w_all, c2h, c2l, ls, acc, bk, bk_in, pose_s, pose_in,
          w_send, w_recv, f_send, f_recv,
          rs_send, rs_recv, ag_send, ag_recv,
@@ -66,6 +66,13 @@
     for i in range(1, D):
         pl.semaphore_signal(barrier, inc=1, device_id={"dom": lax.rem(d + i, D)},
                             device_id_type=pl.DeviceIdType.MESH)
+
+    fetches = [pltpu.make_async_copy(src, dst, in_sem.at[k]) for k, (src, dst) in enumerate(
+        ((bins_hbm, bins), (cls_hbm, cls), (obs_hbm, obs), (ctf_hbm, ctf), (vol_hbm, vol)))]
+    for fetch in fetches:
+        fetch.start()
+    for fetch in fetches[:4]:
+        fetch.wait()
 
     rows = iota((PART, EXT), 0)
     lanes = iota((PART, EXT), 1)
@@ -85,13 +92,6 @@
     extra = jnp.where(lanes == NCTF, bin_col.astype(F32), cls_hot)
     w_all[d, :, WC:] = extra.astype(BF16)
 
-    pl.semaphore_wait(barrier, (G - 1) + (D - 1))
-
-    for i in range(1, D // 2):
-        to = lax.rem(zpos + i, D // 2) * 2 + core
-        dom_copy(w_all.at[d], w_all.at[d], w_send.at[i], w_recv.at[d], to).start()
-    dom_copy(w_all.at[d], w_all.at[d], f_send.at[0], f_recv.at[d], sib).start()
-
     square = table * table
     high = square.astype(BF16)
     c2h[...] = jnp.zeros_like(c2h)
@@ -99,6 +99,7 @@
     c2h[:NCTF, :] = high
     c2l[:NCTF, :] = (square - high.astype(F32)).astype(BF16)
 
+    fetches[4].wait()
     for r in range(R):
         plane_rows = vol[:, r, :]
         coarse = plane_rows.astype(BF16)
@@ -147,6 +148,13 @@
 
     lax.fori_loop(0, NB_DEV, extract, 0)
 
+    pl.semaphore_wait(barrier, (G - 1) + (D - 1))
+
+    for i in range(1, D // 2):
+        to = lax.rem(zpos + i, D // 2) * 2 + core
+        dom_copy(w_all.at[d], w_all.at[d], w_send.at[i], w_recv.at[d], to).start()
+    dom_copy(w_all.at[d], w_all.at[d], f_send.at[0], f_recv.at[d], sib).start()
+
     offset = 4 * core
     mine = lax.rem(g - offset + G, G)
     reduces = mine < NCH
@@ -326,14 +334,20 @@
 
 def local(volume, observed, ctf_table, ctf_class, bin_ids):
     vmem = pl.BlockSpec(memory_space=pltpu.VMEM)
-    smem = pl.BlockSpec(memory_space=pltpu.SMEM)
+    hbm = pl.BlockSpec(memory_space=pltpu.HBM)
     dma = pltpu.SemaphoreType.DMA
     pose, back = pl.pallas_call(
         body,
         out_shape=(jax.ShapeDtypeStruct((1, PART), F32), jax.ShapeDtypeStruct((3, R, X), F32)),
-        in_specs=[vmem, vmem, vmem, smem, smem],
+        in_specs=[hbm] * 5,
         out_specs=(vmem, vmem),
         scratch_shapes=[
+            pltpu.VMEM((SLAB, R, X), F32),
+            pltpu.VMEM((PART, R, U), BF16),
+            pltpu.VMEM((NCTF, 2, U), F32),
+            pltpu.SMEM((PART,), jnp.int32),
+            pltpu.SMEM((PART,), jnp.int32),
+            dma((5,)),
             pltpu.VMEM((2 * R * SLAB, X), BF16),
             pltpu.VMEM((NB_DEV, X, 2 * U), BF16),
             pltpu.VMEM((X, 2 * U), BF16),
@@ -358,7 +372,7 @@
             pltpu.VMEM((D, 1, ALLP), F32),
         ] + [dma((16,))] * 16,
         compiler_params=pltpu.CompilerParams(
-            collective_id=0, has_side_effects=True, vmem_limit_bytes=32 << 20),
+            collective_id=0, has_side_effects=True, vmem_limit_bytes=60 << 20),
         name="tilt_refine",
     )(volume, observed, ctf_table, ctf_class, bin_ids)
     return (pose.reshape(PART), back)

time: 57.6 us -> 54.1 us (0.939)
  local copies, waits for them, and re-layouts: 5.07 us -> 2.47 us
  Pallas kernels: 51.7 us -> 50.8 us
    unnamed x12 -> x4, local copies, waits for them, and re-layouts: 5.07 us -> 2.47 us
    pallas_call x1, Pallas kernels: 51.7 us -> 50.8 us  [local(): pl.pallas_call(body, out_shape=(jax.ShapeDtypeStruct((1, PART), F32), jax...]
where the time goes in v2:
time: 54.1 us; the launch traced here: 53.9 us
  Pallas kernels  50.8 us (94%)
  local copies, waits for them, and re-layouts  2.47 us (5%)
  between operations  0.65 us (1%)
    pallas_call x1, Pallas kernels, local(): pl.pallas_call(body, out_shape=(jax.ShapeDtypeStruct((1, PART), F32), jax...  50.8 us
    unnamed x4, local copies, waits for them, and re-layouts  2.47 us

profile of v2, /device:TPU:1, one launch (start us, length us, event | category | flops | bytes accessed | tf_op | source)
XLA Modules:
  0.0 53.9 jit_solution(1410893909044913162)
XLA Ops:
  0.6 50.8 %tilt_refine.1 = (f32[1,16]{1,0:T(1,128)}, f32[3,4,384]{2,1,0:T(4,128)}) custom-call(f32[48,4,384]{2,1,0:T(4,128)} %vol_hbm.1, bf16[16,4,384]{2,1,0:T(4,128)(2,1)} %obs_hbm.1, f32[32,2,384]{2,1,0:T(2,128)} %ctf_hbm.1, s32[16]{0:T(128)} %cls_hbm.1, s32[16]{0:T(128)} %bins_hbm.1), custom_call_target="tpu_custom_call" | custom-call | tf_op jit(solution)/shard_map/tilt_refine/pallas_call | solution.py:339
  51.4 0.0 copy-start
  51.4 0.6 %copy-done = f32[1,16]{1,0:T(1,128)S(1)} copy-done((f32[1,16]{1,0:T(1,128)S(1)}, f32[1,16]{1,0:T(1,128)}, u32[]{:S(2)}) %copy-start) | copy-done | bytes 88
  52.0 0.5 copy.9
  52.6 1.3 %copy.10 = f32[3,4,384]{2,1,0:T(4,128)} copy(f32[3,4,384]{2,1,0:T(4,128)} %get-tuple-element.9) | data formatting | bytes 36864
Async XLA Ops:
  51.4 0.6 %copy-start = (f32[1,16]{1,0:T(1,128)S(1)}, f32[1,16]{1,0:T(1,128)}, u32[]{:S(2)}) copy-start(f32[1,16]{1,0:T(1,128)} %get-tuple-element.4) | copy-start | bytes 196

commit v3 on v2

v3 whole, which is shorter than its diff:
```python
import math

import jax
import jax.numpy as jnp
from jax import lax
from jax.experimental import pallas as pl
from jax.experimental.pallas import tpu as pltpu
from jax.sharding import PartitionSpec as P

NZ = 768
NB = 128
NB_DEV = 8
NCTF = 32
ITERS = 3
EPS = 1e-05
G = 16
D = 16
SLAB = 48
R = 4
X = 384
U = 384
PART = 16
ALLP = PART * D
WC = R * U
EXT = 128
BLOCKS = 3
BL = 128
F32 = jnp.float32
BF16 = jnp.bfloat16
NT = (((1,), (1,)), ((), ()))


def slab_spans():
    spans = []
    for j in range(BLOCKS):
        row = []
        for k in range(D):
            sines = [math.sin(-0.5 * math.pi + math.pi * (b + 0.5) / NB)
                     for b in range(k * NB_DEV, (k + 1) * NB_DEV)]
            centres = [0.5 * NZ + u * sine for sine in sines for u in (j * BL, j * BL + BL - 1)]
            first = math.floor(min(centres) - 1e-3)
            last = math.floor(max(centres) + 1e-3) + 1
            row.append((max(first, 0) // SLAB, min(last, NZ - 1) // SLAB))
        spans.append(row)
    return spans


def iota(shape, dim):
    return lax.broadcasted_iota(jnp.int32, shape, dim)


def gz_copy(src, dst, send, recv, to):
    return pltpu.make_async_remote_copy(
        src_ref=src, dst_ref=dst, send_sem=send, recv_sem=recv,
        device_id={"gz": to}, device_id_type=pl.DeviceIdType.MESH)


def dom_copy(src, dst, send, recv, to):
    return pltpu.make_async_remote_copy(
        src_ref=src, dst_ref=dst, send_sem=send, recv_sem=recv,
        device_id={"dom": to}, device_id_type=pl.DeviceIdType.MESH)


def body(vol_hbm, obs_hbm, ctf_hbm, cls_hbm, bins_hbm, pose_out, back_out,
         vol, obs, ctf, cls, bins, in_sem, vb, kt, kz, kzd, sc, sp, spb, sp_in, s_all, ss, ss_in, t32,
         w_all, c2h, c2l, acc, bk, bk_in, pose_s, pose_in,
         w_send, w_recv, f_send, f_recv,
         rs_send, rs_recv, rs2_send, rs2_recv, b_send, b_recv, p_send, p_recv):
    g = lax.axis_index("gz")
    d = lax.axis_index("dom")
    core = lax.rem(d, 2)
    zpos = lax.div(d, 2)
    sib = d + 1 - 2 * core
    first_bin = d * NB_DEV

    barrier = pltpu.get_barrier_semaphore()
    for i in range(1, D):
        pl.semaphore_signal(barrier, inc=1, device_id={"dom": lax.rem(d + i, D)},
                            device_id_type=pl.DeviceIdType.MESH)
    for i in range(1, G):
        pl.semaphore_signal(barrier, inc=1, device_id={"gz": lax.rem(g + i, G)},
                            device_id_type=pl.DeviceIdType.MESH)

    low, high_slab = [], []
    for row in slab_spans():
        least, most = jnp.int32(row[0][0]), jnp.int32(row[0][1])
        for k in range(1, D):
            least = jnp.where(d == k, row[k][0], least)
            most = jnp.where(d == k, row[k][1], most)
        low.append(least)
        high_slab.append(most)

    def active(j, slab):
        return (low[j] <= slab) & (slab <= high_slab[j])

    fetches = [pltpu.make_async_copy(src, dst, in_sem.at[k]) for k, (src, dst) in enumerate(
        ((bins_hbm, bins), (cls_hbm, cls), (obs_hbm, obs), (ctf_hbm, ctf), (vol_hbm, vol)))]
    for fetch in fetches:
        fetch.start()
    for fetch in fetches[:4]:
        fetch.wait()

    rows = iota((PART, EXT), 0)
    lanes = iota((PART, EXT), 1)
    cls_col = jnp.zeros((PART, EXT), jnp.int32)
    bin_col = jnp.zeros((PART, EXT), jnp.int32)
    for i in range(PART):
        cls_col = jnp.where(rows == i, cls[i], cls_col)
        bin_col = jnp.where(rows == i, bins[i], bin_col)
    cls_hot = (cls_col == lanes).astype(F32)
    table = jnp.concatenate([ctf[:, 0, :], ctf[:, 1, :]], 1)
    contrast = jnp.dot(cls_hot[:, :NCTF], table, precision=lax.Precision.HIGHEST,
                       preferred_element_type=F32)
    for r in range(R):
        y = r % 2
        image = obs[:, r, :].astype(F32)
        w_all[d, :, r * U:(r + 1) * U] = (image * contrast[:, y * U:(y + 1) * U]).astype(BF16)
    extra = jnp.where(lanes == NCTF, bin_col.astype(F32), cls_hot)
    w_all[d, :, WC:] = extra.astype(BF16)

    square = table * table
    high = square.astype(BF16)
    c2h[...] = jnp.zeros_like(c2h)
    c2l[...] = jnp.zeros_like(c2l)
    c2h[:NCTF, :] = high
    c2l[:NCTF, :] = (square - high.astype(F32)).astype(BF16)

    fetches[4].wait()
    for r in range(R):
        plane_rows = vol[:, r, :]
        coarse = plane_rows.astype(BF16)
        vb[r * SLAB:(r + 1) * SLAB, :] = coarse
        vb[(R + r) * SLAB:(R + r + 1) * SLAB, :] = (plane_rows - coarse.astype(F32)).astype(BF16)
    bin_index = (first_bin + iota((NB_DEV, 128), 0)).astype(F32)
    theta = -0.5 * math.pi + math.pi * (bin_index + 0.5) / NB
    sc[:NB_DEV, :] = jnp.sin(theta)
    sc[NB_DEV:, :] = jnp.cos(theta)

    for j in range(BLOCKS):
        wide = BL * (j + 1)
        radius = (BL * j + iota((1, BL), 1)).astype(F32)
        plane = (g * SLAB + iota((SLAB, BL), 0)).astype(F32)
        column = iota((wide, BL), 0).astype(F32)

        def extract(b, carry, j=j, wide=wide, radius=radius, plane=plane, column=column):
            sine = sc[pl.ds(b, 1), :]
            cosine = sc[pl.ds(NB_DEV + b, 1), :]
            tx = column - radius * cosine
            fx = jnp.maximum(1.0 - tx * tx, 0.0)
            kx = jnp.concatenate([fx * fx, (tx * fx) * (radius * sine * (-4.0 / U))], 1)
            kx_high = kx.astype(BF16)
            kt[b, :wide, 2 * BL * j:2 * BL * (j + 1)] = kx_high
            kx_low = (kx - kx_high.astype(F32)).astype(BF16)
            tz = plane - (0.5 * NZ + radius * sine)
            fz = jnp.maximum(1.0 - tz * tz, 0.0)
            wz = fz * fz
            wd = (tz * fz) * (radius * cosine * (4.0 / U))
            kz[b, :, BL * j:BL * (j + 1)] = wz
            kzd[b, :, BL * j:BL * (j + 1)] = wd
            stacked = jnp.dot(vb[:, :wide], kx_high, preferred_element_type=F32)
            both = stacked[:R * SLAB] + stacked[R * SLAB:] + jnp.dot(
                vb[:R * SLAB, :wide], kx_low, preferred_element_type=F32)
            for r in range(R):
                direct = both[r * SLAB:(r + 1) * SLAB, :BL]
                tilted = both[r * SLAB:(r + 1) * SLAB, BL:]
                sp[j, pl.ds(r * 8 + b, 1), :] = jnp.sum(direct * wz, axis=0, keepdims=True)
                sp[j, pl.ds(32 + r * 8 + b, 1), :] = jnp.sum(
                    direct * wd + tilted * wz, axis=0, keepdims=True)
            return carry

        @pl.when(active(j, g))
        def _(j=j, extract=extract):
            lax.fori_loop(0, NB_DEV, extract, 0)
            spb[j] = sp[j].astype(BF16)

    pl.semaphore_wait(barrier, (G - 1) + (D - 1))

    for i in range(1, D // 2):
        to = lax.rem(zpos + i, D // 2) * 2 + core
        dom_copy(w_all.at[d], w_all.at[d], w_send.at[i], w_recv.at[d], to).start()
    dom_copy(w_all.at[d], w_all.at[d], f_send.at[0], f_recv.at[d], sib).start()

    for j in range(BLOCKS):
        @pl.when(active(j, g))
        def _(j=j):
            for i in range(1, G):
                gz_copy(spb.at[j], sp_in.at[j, g], rs_send.at[j, i], rs_recv.at[j, g], lax.rem(g + i, G)).start()
            sp_in[j, g] = spb[j]

    for i in range(1, D // 2):
        frm = lax.rem(zpos + i, D // 2) * 2 + core
        dom_copy(w_all.at[frm], w_all.at[frm], w_recv.at[frm], w_recv.at[frm], sib).wait_recv()
        dom_copy(w_all.at[frm], w_all.at[frm], f_send.at[i], f_recv.at[frm], sib).start()

    for j in range(BLOCKS):
        def gather(frm, total, j=j):
            @pl.when(frm != g)
            def _():
                gz_copy(spb.at[j], sp_in.at[j, frm], rs_recv.at[j, frm], rs_recv.at[j, frm],
                        lax.rem(g + 1, G)).wait_recv()
            return total + sp_in[j, frm].astype(F32)

        s_all[j] = lax.fori_loop(low[j], high_slab[j] + 1, gather, jnp.zeros((64, BL), F32))

    def rows_of(kind, r):
        at = 32 * kind + 8 * r
        rounded = jnp.concatenate([s_all[j, at:at + 8, :] for j in range(BLOCKS)], 1)
        return rounded.astype(BF16).astype(F32)

    lead = [rows_of(0, r) for r in range(R)]
    slope = [rows_of(1, r) for r in range(R)]
    curve = jnp.concatenate([slope[y] * slope[y] + slope[y + 2] * slope[y + 2] for y in range(2)], 1)
    cross = jnp.concatenate([lead[y] * slope[y] + lead[y + 2] * slope[y + 2] for y in range(2)], 1)
    quad = jnp.concatenate([curve, cross], 0)
    quad_high = quad.astype(BF16)
    quad_low = (quad - quad_high.astype(F32)).astype(BF16)
    first = lax.dot_general(jnp.concatenate([quad_high, quad_low], 0), c2h[...], NT,
                            preferred_element_type=F32)
    tables = first[:16] + first[16:] + lax.dot_general(quad_high, c2l[...], NT,
                                                       preferred_element_type=F32)
    tables_high = tables.astype(BF16)
    tables_low = (tables - tables_high.astype(F32)).astype(BF16)
    pick = (iota((8, EXT), 1) == NCTF).astype(F32).astype(BF16)
    zero = jnp.zeros((8, EXT), BF16)
    lookup = jnp.concatenate([tables_high, tables_low, pick, zero], 0)
    slope_rows = jnp.concatenate(slope, 1).astype(BF16)

    for i in range(0, D // 2):
        frm = lax.rem(zpos + i, D // 2) * 2 + 1 - core
        dom_copy(w_all.at[frm], w_all.at[frm], f_recv.at[frm], f_recv.at[frm], sib).wait_recv()

    images = w_all[:, :, :WC].reshape(ALLP, WC)
    marks = w_all[:, :, WC:].reshape(ALLP, EXT)
    looked = lax.dot_general(lookup, marks, NT, preferred_element_type=F32)
    along = lax.dot_general(slope_rows, images, NT, preferred_element_type=F32)
    held = looked[0:8] + looked[16:24]
    crossed = looked[8:16] + looked[24:32]
    own = (first_bin + iota((8, ALLP), 0)).astype(F32) == looked[32:40]
    mask = own.astype(F32)
    power = jnp.sum(mask * held, axis=0, keepdims=True)
    match = jnp.sum(mask * (along - crossed), axis=0, keepdims=True)
    curvature = power + EPS
    shift = jnp.zeros_like(power)
    for _ in range(ITERS):
        shift = shift + 0.5 * (match - shift * power) / curvature
    pose_s[...] = shift * jnp.sqrt(curvature)
    moved = mask * shift
    moved_high = moved.astype(BF16)
    moved_low = (moved - moved_high.astype(F32)).astype(BF16)
    spread = jnp.concatenate([mask.astype(BF16), moved_high, moved_low, jnp.zeros((8, ALLP), BF16)], 0)
    sums = jnp.dot(spread, images, preferred_element_type=F32)
    for r in range(R):
        part = sums[:, r * U:(r + 1) * U]
        part = jnp.concatenate([part[:8], part[8:16] + part[16:24]], 0).astype(BF16)
        for j in range(BLOCKS):
            ss[j, 16 * r:16 * (r + 1), :] = part[:, BL * j:BL * (j + 1)]

    for i in range(1, G):
        to = lax.rem(g + i, G)
        for j in range(BLOCKS):
            @pl.when(active(j, to))
            def _(i=i, j=j, to=to):
                gz_copy(ss.at[j], ss_in.at[j, g], rs2_send.at[j, i], rs2_recv.at[j, g], to).start()
    for i in range(1, D):
        to = lax.rem(d + i, D)
        dom_copy(pose_s, pose_in.at[d], p_send.at[i], p_recv.at[d], to).start()

    acc[...] = jnp.zeros_like(acc)
    row = iota((256, R * SLAB), 0)
    within = lax.rem(row, 16)
    source = lax.rem(row, 4) * SLAB + 3 * lax.div(row, 16) + lax.div(within, 4)
    order = ((iota((256, R * SLAB), 1) == source) & (within < 12)).astype(F32).astype(BF16)

    for j in reversed(range(BLOCKS)):
        wide = BL * (j + 1)

        def spread_back(b, carry, j=j, wide=wide):
            wz = kz[b, :, BL * j:BL * (j + 1)]
            wd = kzd[b, :, BL * j:BL * (j + 1)]
            parts = []
            for r in range(R):
                plain = t32[j, pl.ds(16 * r + b, 1), :]
                sloped = t32[j, pl.ds(16 * r + 8 + b, 1), :]
                parts.append(jnp.concatenate([wz * plain + wd * sloped, wz * sloped], 1))
            left = jnp.concatenate(parts, 0)
            left_high = left.astype(BF16)
            left_low = (left - left_high.astype(F32)).astype(BF16)
            both = lax.dot_general(
                jnp.concatenate([left_high, left_low], 0),
                kt[b, :wide, 2 * BL * j:2 * BL * (j + 1)], NT, preferred_element_type=F32)
            acc[:, :wide] += both[:R * SLAB] + both[R * SLAB:]
            return carry

        @pl.when(active(j, g))
        def _(j=j, spread_back=spread_back):
            ss_in[j, g] = ss[j]
            for i in range(1, G):
                frm = lax.rem(g + i, G)
                gz_copy(ss.at[j], ss_in.at[j, frm], rs2_recv.at[j, frm], rs2_recv.at[j, frm], frm).wait_recv()
            total = ss_in[j, 0].astype(F32)
            for i in range(1, G):
                total = total + ss_in[j, i].astype(F32)
            t32[j] = total
            lax.fori_loop(0, NB_DEV, spread_back, 0)

        ordered = jnp.dot(order, acc[:, BL * j:BL * (j + 1)].astype(BF16), preferred_element_type=F32)
        bk[j] = ordered.astype(BF16).reshape(D, 16, BL)
        for i in range(1, D):
            to = lax.rem(d + i, D)
            dom_copy(bk.at[j, to], bk_in.at[j, d], b_send.at[j, i], b_recv.at[j, d], to).start()

    pose_in[d] = pose_s[...]
    for i in range(1, D):
        frm = lax.rem(d + i, D)
        dom_copy(pose_s, pose_in.at[frm], p_recv.at[frm], p_recv.at[frm], frm).wait_recv()
    pose = pose_in[0]
    for i in range(1, D):
        pose = pose + pose_in[i]
    lane = iota((8, ALLP), 1)
    kept = jnp.where(lax.div(lane, PART) == d, pose, 0.0)
    choose = (lax.rem(iota((ALLP, 128), 0), PART) == iota((ALLP, 128), 1)).astype(F32)
    picked = jnp.dot(kept, choose, precision=lax.Precision.HIGHEST, preferred_element_type=F32)
    pose_out[...] = picked[0:1, :PART]

    for j in reversed(range(BLOCKS)):
        bk_in[j, d] = bk[j, d]
        for i in range(1, D):
            frm = lax.rem(d + i, D)
            dom_copy(bk.at[j, 0], bk_in.at[j, frm], b_recv.at[j, frm], b_recv.at[j, frm], frm).wait_recv()
        total = bk_in[j, 0].astype(F32)
        for i in range(1, D):
            total = total + bk_in[j, i].astype(F32)
        for k in range(3):
            back_out[k, :, BL * j:BL * (j + 1)] = total[4 * k:4 * k + 4]

    for i in range(1, G):
        to = lax.rem(g + i, G)
        for j in range(BLOCKS):
            @pl.when(active(j, g))
            def _(i=i, j=j, to=to):
                gz_copy(spb.at[j], sp_in.at[j, g], rs_send.at[j, i], rs_send.at[j, i], to).wait_send()

            @pl.when(active(j, to))
            def _(i=i, j=j, to=to):
                gz_copy(ss.at[j], ss_in.at[j, g], rs2_send.at[j, i], rs2_send.at[j, i], to).wait_send()
    for i in range(1, D // 2):
        dom_copy(w_all.at[d], w_all.at[d], w_send.at[i], w_send.at[i], sib).wait_send()
    for i in range(0, D // 2):
        dom_copy(w_all.at[d], w_all.at[d], f_send.at[i], f_send.at[i], sib).wait_send()
    for i in range(1, D):
        for j in range(BLOCKS):
            dom_copy(bk.at[j, 0], bk_in.at[j, d], b_send.at[j, i], b_send.at[j, i], sib).wait_send()
        dom_copy(pose_s, pose_in.at[d], p_send.at[i], p_send.at[i], sib).wait_send()


def local(volume, observed, ctf_table, ctf_class, bin_ids):
    vmem = pl.BlockSpec(memory_space=pltpu.VMEM)
    hbm = pl.BlockSpec(memory_space=pltpu.HBM)
    dma = pltpu.SemaphoreType.DMA
    pose, back = pl.pallas_call(
        body,
        out_shape=(jax.ShapeDtypeStruct((1, PART), F32), jax.ShapeDtypeStruct((3, R, X), F32)),
        in_specs=[hbm] * 5,
        out_specs=(vmem, vmem),
        scratch_shapes=[
            pltpu.VMEM((SLAB, R, X), F32),
            pltpu.VMEM((PART, R, U), BF16),
            pltpu.VMEM((NCTF, 2, U), F32),
            pltpu.SMEM((PART,), jnp.int32),
            pltpu.SMEM((PART,), jnp.int32),
            dma((5,)),
            pltpu.VMEM((2 * R * SLAB, X), BF16),
            pltpu.VMEM((NB_DEV, X, 2 * U), BF16),
            pltpu.VMEM((NB_DEV, SLAB, U), F32),
            pltpu.VMEM((NB_DEV, SLAB, U), F32),
            pltpu.VMEM((2 * NB_DEV, 128), F32),
            pltpu.VMEM((BLOCKS, 64, BL), F32),
            pltpu.VMEM((BLOCKS, 64, BL), BF16),
            pltpu.VMEM((BLOCKS, G, 64, BL), BF16),
            pltpu.VMEM((BLOCKS, 64, BL), F32),
            pltpu.VMEM((BLOCKS, 64, BL), BF16),
            pltpu.VMEM((BLOCKS, G, 64, BL), BF16),
            pltpu.VMEM((BLOCKS, 64, BL), F32),
            pltpu.VMEM((D, PART, WC + EXT), BF16),
            pltpu.VMEM((EXT, 2 * U), BF16),
            pltpu.VMEM((EXT, 2 * U), BF16),
            pltpu.VMEM((R * SLAB, X), F32),
            pltpu.VMEM((BLOCKS, D, 16, BL), BF16),
            pltpu.VMEM((BLOCKS, D, 16, BL), BF16),
            pltpu.VMEM((1, ALLP), F32),
            pltpu.VMEM((D, 1, ALLP), F32),
        ] + [dma((16,))] * 4 + [dma((BLOCKS, 16))] * 6 + [dma((16,))] * 2,
        compiler_params=pltpu.CompilerParams(
            collective_id=0, has_side_effects=True, vmem_limit_bytes=60 << 20),
        name="tilt_refine",
    )(volume, observed, ctf_table, ctf_class, bin_ids)
    return (pose.reshape(PART), back)


def solution(mesh):
    return jax.shard_map(
        local,
        mesh=mesh,
        in_specs=(
            P("gz", None, None),
            P(("gz", "dom"), None, None),
            P(),
            P(("gz", "dom")),
            P(("gz", "dom")),
        ),
        out_specs=(P(("gz", "dom")), P(("gz", "dom"), None, None)),
        check_vma=False,
    )
```

time: 54.1 us -> 50.1 us (0.926)
  the two profiles are of different devices: /device:TPU:1 before, /device:TPU:17 now
where the time goes in v3:
time: 50.1 us; the launch traced here: 49.9 us
  Pallas kernels  46.8 us (93%)
  local copies, waits for them, and re-layouts  2.47 us (5%)
  between operations  0.65 us (1%)
    pallas_call x1, Pallas kernels, local(): pl.pallas_call(body, out_shape=(jax.ShapeDtypeStruct((1, PART), F32), jax...  46.8 us
    unnamed x4, local copies, waits for them, and re-layouts  2.47 us

profile of v3, /device:TPU:17, one launch (start us, length us, event | category | flops | bytes accessed | tf_op | source)
XLA Modules:
  0.0 49.9 jit_solution(18418314655127104499)
XLA Ops:
  0.6 46.8 %tilt_refine.1 = (f32[1,16]{1,0:T(1,128)}, f32[3,4,384]{2,1,0:T(4,128)}) custom-call(f32[48,4,384]{2,1,0:T(4,128)} %vol_hbm.1, bf16[16,4,384]{2,1,0:T(4,128)(2,1)} %obs_hbm.1, f32[32,2,384]{2,1,0:T(2,128)} %ctf_hbm.1, s32[16]{0:T(128)} %cls_hbm.1, s32[16]{0:T(128)} %bins_hbm.1), custom_call_target="tpu_custom_call" | custom-call | tf_op jit(solution)/shard_map/tilt_refine/pallas_call | solution.py:360
  47.4 0.0 copy-start
  47.4 0.6 %copy-done = f32[1,16]{1,0:T(1,128)S(1)} copy-done((f32[1,16]{1,0:T(1,128)S(1)}, f32[1,16]{1,0:T(1,128)}, u32[]{:S(2)}) %copy-start) | copy-done | bytes 88
  48.1 0.5 %copy.9 = f32[16]{0:T(128)} copy(f32[16]{0:T(128)S(1)} %bitcast.1) | data formatting | bytes 128
  48.6 1.3 %copy.10 = f32[3,4,384]{2,1,0:T(4,128)} copy(f32[3,4,384]{2,1,0:T(4,128)} %get-tuple-element.9) | data formatting | bytes 36864
Async XLA Ops:
  47.4 0.6 %copy-start = (f32[1,16]{1,0:T(1,128)S(1)}, f32[1,16]{1,0:T(1,128)}, u32[]{:S(2)}) copy-start(f32[1,16]{1,0:T(1,128)} %get-tuple-element.4) | copy-start | bytes 196

commit v4 on v3

--- a/solution.py
+++ b/solution.py
@@ -25,6 +25,8 @@
 EXT = 128
 BLOCKS = 3
 BL = 128
+PAIRS = 4
+UNITS = [(k, j) for j in range(BLOCKS) for k in range(PAIRS)]
 F32 = jnp.float32
 BF16 = jnp.bfloat16
 NT = (((1,), (1,)), ((), ()))
@@ -32,11 +34,11 @@
 
 def slab_spans():
     spans = []
-    for j in range(BLOCKS):
+    for k, j in UNITS:
         row = []
-        for k in range(D):
-            sines = [math.sin(-0.5 * math.pi + math.pi * (b + 0.5) / NB)
-                     for b in range(k * NB_DEV, (k + 1) * NB_DEV)]
+        for dom in range(D):
+            sines = [math.sin(-0.5 * math.pi + math.pi * (2 * (dom + D * k) + i + 0.5) / NB)
+                     for i in range(2)]
             centres = [0.5 * NZ + u * sine for sine in sines for u in (j * BL, j * BL + BL - 1)]
             first = math.floor(min(centres) - 1e-3)
             last = math.floor(max(centres) + 1e-3) + 1
@@ -62,7 +64,7 @@
 
 
 def body(vol_hbm, obs_hbm, ctf_hbm, cls_hbm, bins_hbm, pose_out, back_out,
-         vol, obs, ctf, cls, bins, in_sem, vb, kt, kz, kzd, sc, sp, spb, sp_in, s_all, ss, ss_in, t32,
+         vol, obs, ctf, cls, bins, in_sem, vb, kt, kz, kzd, sc, sp, spb, sp_in, s_all, sf, ss, ss_in,
          w_all, c2h, c2l, acc, bk, bk_in, pose_s, pose_in,
          w_send, w_recv, f_send, f_recv,
          rs_send, rs_recv, rs2_send, rs2_recv, b_send, b_recv, p_send, p_recv):
@@ -71,7 +73,10 @@
     core = lax.rem(d, 2)
     zpos = lax.div(d, 2)
     sib = d + 1 - 2 * core
-    first_bin = d * NB_DEV
+
+    def bin_of(slot):
+        return 2 * d + 2 * D * lax.div(slot, 2) + lax.rem(slot, 2)
+
 
     barrier = pltpu.get_barrier_semaphore()
     for i in range(1, D):
@@ -81,17 +86,17 @@
         pl.semaphore_signal(barrier, inc=1, device_id={"gz": lax.rem(g + i, G)},
                             device_id_type=pl.DeviceIdType.MESH)
 
-    low, high_slab = [], []
+    low, top = [], []
     for row in slab_spans():
         least, most = jnp.int32(row[0][0]), jnp.int32(row[0][1])
         for k in range(1, D):
             least = jnp.where(d == k, row[k][0], least)
             most = jnp.where(d == k, row[k][1], most)
         low.append(least)
-        high_slab.append(most)
-
-    def active(j, slab):
-        return (low[j] <= slab) & (slab <= high_slab[j])
+        top.append(most)
+
+    def active(n, slab):
+        return (low[n] <= slab) & (slab <= top[n])
 
     fetches = [pltpu.make_async_copy(src, dst, in_sem.at[k]) for k, (src, dst) in enumerate(
         ((bins_hbm, bins), (cls_hbm, cls), (obs_hbm, obs), (ctf_hbm, ctf), (vol_hbm, vol)))]
@@ -131,7 +136,7 @@
         coarse = plane_rows.astype(BF16)
         vb[r * SLAB:(r + 1) * SLAB, :] = coarse
         vb[(R + r) * SLAB:(R + r + 1) * SLAB, :] = (plane_rows - coarse.astype(F32)).astype(BF16)
-    bin_index = (first_bin + iota((NB_DEV, 128), 0)).astype(F32)
+    bin_index = bin_of(iota((NB_DEV, 128), 0)).astype(F32)
     theta = -0.5 * math.pi + math.pi * (bin_index + 0.5) / NB
     sc[:NB_DEV, :] = jnp.sin(theta)
     sc[NB_DEV:, :] = jnp.cos(theta)
@@ -142,36 +147,41 @@
         plane = (g * SLAB + iota((SLAB, BL), 0)).astype(F32)
         column = iota((wide, BL), 0).astype(F32)
 
-        def extract(b, carry, j=j, wide=wide, radius=radius, plane=plane, column=column):
-            sine = sc[pl.ds(b, 1), :]
-            cosine = sc[pl.ds(NB_DEV + b, 1), :]
-            tx = column - radius * cosine
-            fx = jnp.maximum(1.0 - tx * tx, 0.0)
-            kx = jnp.concatenate([fx * fx, (tx * fx) * (radius * sine * (-4.0 / U))], 1)
-            kx_high = kx.astype(BF16)
-            kt[b, :wide, 2 * BL * j:2 * BL * (j + 1)] = kx_high
-            kx_low = (kx - kx_high.astype(F32)).astype(BF16)
-            tz = plane - (0.5 * NZ + radius * sine)
-            fz = jnp.maximum(1.0 - tz * tz, 0.0)
-            wz = fz * fz
-            wd = (tz * fz) * (radius * cosine * (4.0 / U))
-            kz[b, :, BL * j:BL * (j + 1)] = wz
-            kzd[b, :, BL * j:BL * (j + 1)] = wd
-            stacked = jnp.dot(vb[:, :wide], kx_high, preferred_element_type=F32)
-            both = stacked[:R * SLAB] + stacked[R * SLAB:] + jnp.dot(
-                vb[:R * SLAB, :wide], kx_low, preferred_element_type=F32)
-            for r in range(R):
-                direct = both[r * SLAB:(r + 1) * SLAB, :BL]
-                tilted = both[r * SLAB:(r + 1) * SLAB, BL:]
-                sp[j, pl.ds(r * 8 + b, 1), :] = jnp.sum(direct * wz, axis=0, keepdims=True)
-                sp[j, pl.ds(32 + r * 8 + b, 1), :] = jnp.sum(
-                    direct * wd + tilted * wz, axis=0, keepdims=True)
-            return carry
-
-        @pl.when(active(j, g))
-        def _(j=j, extract=extract):
-            lax.fori_loop(0, NB_DEV, extract, 0)
-            spb[j] = sp[j].astype(BF16)
+        def extract(n, k, j=j, wide=wide, radius=radius, plane=plane, column=column):
+            for i in range(2):
+                b = 2 * k + i
+                sine = sc[b:b + 1, :]
+                cosine = sc[NB_DEV + b:NB_DEV + b + 1, :]
+                tx = column - radius * cosine
+                fx = jnp.maximum(1.0 - tx * tx, 0.0)
+                kx = jnp.concatenate([fx * fx, (tx * fx) * (radius * sine * (-4.0 / U))], 1)
+                kx_high = kx.astype(BF16)
+                kt[b, :wide, 2 * BL * j:2 * BL * (j + 1)] = kx_high
+                kx_low = (kx - kx_high.astype(F32)).astype(BF16)
+                tz = plane - (0.5 * NZ + radius * sine)
+                fz = jnp.maximum(1.0 - tz * tz, 0.0)
+                wz = fz * fz
+                wd = (tz * fz) * (radius * cosine * (4.0 / U))
+                kz[b, :, BL * j:BL * (j + 1)] = wz
+                kzd[b, :, BL * j:BL * (j + 1)] = wd
+                stacked = jnp.dot(vb[:, :wide], kx_high, preferred_element_type=F32)
+                both = stacked[:R * SLAB] + stacked[R * SLAB:] + jnp.dot(
+                    vb[:R * SLAB, :wide], kx_low, preferred_element_type=F32)
+                for r in range(R):
+                    direct = both[r * SLAB:(r + 1) * SLAB, :BL]
+                    tilted = both[r * SLAB:(r + 1) * SLAB, BL:]
+                    at = 2 * r + i
+                    sp[n, at:at + 1, :] = jnp.sum(direct * wz, axis=0, keepdims=True)
+                    sp[n, 8 + at:8 + at + 1, :] = jnp.sum(
+                        direct * wd + tilted * wz, axis=0, keepdims=True)
+            spb[n] = sp[n].astype(BF16)
+
+        for k in range(PAIRS):
+            n = UNITS.index((k, j))
+
+            @pl.when(active(n, g))
+            def _(n=n, k=k, extract=extract):
+                extract(n, k)
 
     pl.semaphore_wait(barrier, (G - 1) + (D - 1))
 
@@ -180,27 +190,29 @@
         dom_copy(w_all.at[d], w_all.at[d], w_send.at[i], w_recv.at[d], to).start()
     dom_copy(w_all.at[d], w_all.at[d], f_send.at[0], f_recv.at[d], sib).start()
 
-    for j in range(BLOCKS):
-        @pl.when(active(j, g))
-        def _(j=j):
+    for n in range(len(UNITS)):
+        @pl.when(active(n, g))
+        def _(n=n):
             for i in range(1, G):
-                gz_copy(spb.at[j], sp_in.at[j, g], rs_send.at[j, i], rs_recv.at[j, g], lax.rem(g + i, G)).start()
-            sp_in[j, g] = spb[j]
+                gz_copy(spb.at[n], sp_in.at[n, g], rs_send.at[n, i], rs_recv.at[n, g], lax.rem(g + i, G)).start()
+            sp_in[n, g] = spb[n]
 
     for i in range(1, D // 2):
         frm = lax.rem(zpos + i, D // 2) * 2 + core
         dom_copy(w_all.at[frm], w_all.at[frm], w_recv.at[frm], w_recv.at[frm], sib).wait_recv()
         dom_copy(w_all.at[frm], w_all.at[frm], f_send.at[i], f_recv.at[frm], sib).start()
 
-    for j in range(BLOCKS):
-        def gather(frm, total, j=j):
+    for n, (k, j) in enumerate(UNITS):
+        def gather(frm, total, n=n):
             @pl.when(frm != g)
             def _():
-                gz_copy(spb.at[j], sp_in.at[j, frm], rs_recv.at[j, frm], rs_recv.at[j, frm],
+                gz_copy(spb.at[n], sp_in.at[n, frm], rs_recv.at[n, frm], rs_recv.at[n, frm],
                         lax.rem(g + 1, G)).wait_recv()
-            return total + sp_in[j, frm].astype(F32)
-
-        s_all[j] = lax.fori_loop(low[j], high_slab[j] + 1, gather, jnp.zeros((64, BL), F32))
+            return total + sp_in[n, frm].astype(F32)
+
+        total = lax.fori_loop(low[n], top[n] + 1, gather, jnp.zeros((16, BL), F32))
+        for m in range(8):
+            s_all[j, 8 * m + 2 * k:8 * m + 2 * k + 2, :] = total[2 * m:2 * m + 2]
 
     def rows_of(kind, r):
         at = 32 * kind + 8 * r
@@ -235,7 +247,7 @@
     along = lax.dot_general(slope_rows, images, NT, preferred_element_type=F32)
     held = looked[0:8] + looked[16:24]
     crossed = looked[8:16] + looked[24:32]
-    own = (first_bin + iota((8, ALLP), 0)).astype(F32) == looked[32:40]
+    own = bin_of(iota((8, ALLP), 0)).astype(F32) == looked[32:40]
     mask = own.astype(F32)
     power = jnp.sum(mask * held, axis=0, keepdims=True)
     match = jnp.sum(mask * (along - crossed), axis=0, keepdims=True)
@@ -251,16 +263,24 @@
     sums = jnp.dot(spread, images, preferred_element_type=F32)
     for r in range(R):
         part = sums[:, r * U:(r + 1) * U]
-        part = jnp.concatenate([part[:8], part[8:16] + part[16:24]], 0).astype(BF16)
-        for j in range(BLOCKS):
-            ss[j, 16 * r:16 * (r + 1), :] = part[:, BL * j:BL * (j + 1)]
-
-    for i in range(1, G):
-        to = lax.rem(g + i, G)
-        for j in range(BLOCKS):
-            @pl.when(active(j, to))
-            def _(i=i, j=j, to=to):
-                gz_copy(ss.at[j], ss_in.at[j, g], rs2_send.at[j, i], rs2_recv.at[j, g], to).start()
+        plain = part[:8]
+        sloped = part[8:16] + part[16:24]
+        for n, (k, j) in enumerate(UNITS):
+            sf[n, 4 * r:4 * r + 2, :] = plain[2 * k:2 * k + 2, BL * j:BL * (j + 1)]
+            sf[n, 4 * r + 2:4 * r + 4, :] = sloped[2 * k:2 * k + 2, BL * j:BL * (j + 1)]
+    ss[...] = sf[...].astype(BF16)
+
+    def each_slab(n, act):
+        def one(to, carry):
+            @pl.when(to != g)
+            def _():
+                act(gz_copy(ss.at[n], ss_in.at[n, g], rs2_send.at[n, to], rs2_recv.at[n, g], to))
+            return carry
+
+        lax.fori_loop(low[n], top[n] + 1, one, 0)
+
+    for n in reversed(range(len(UNITS))):
+        each_slab(n, lambda copy: copy.start())
     for i in range(1, D):
         to = lax.rem(d + i, D)
         dom_copy(pose_s, pose_in.at[d], p_send.at[i], p_recv.at[d], to).start()
@@ -274,34 +294,37 @@
     for j in reversed(range(BLOCKS)):
         wide = BL * (j + 1)
 
-        def spread_back(b, carry, j=j, wide=wide):
-            wz = kz[b, :, BL * j:BL * (j + 1)]
-            wd = kzd[b, :, BL * j:BL * (j + 1)]
-            parts = []
-            for r in range(R):
-                plain = t32[j, pl.ds(16 * r + b, 1), :]
-                sloped = t32[j, pl.ds(16 * r + 8 + b, 1), :]
-                parts.append(jnp.concatenate([wz * plain + wd * sloped, wz * sloped], 1))
-            left = jnp.concatenate(parts, 0)
-            left_high = left.astype(BF16)
-            left_low = (left - left_high.astype(F32)).astype(BF16)
-            both = lax.dot_general(
-                jnp.concatenate([left_high, left_low], 0),
-                kt[b, :wide, 2 * BL * j:2 * BL * (j + 1)], NT, preferred_element_type=F32)
-            acc[:, :wide] += both[:R * SLAB] + both[R * SLAB:]
-            return carry
-
-        @pl.when(active(j, g))
-        def _(j=j, spread_back=spread_back):
-            ss_in[j, g] = ss[j]
+        def spread_back(n, k, j=j, wide=wide):
+            ss_in[n, g] = ss[n]
             for i in range(1, G):
                 frm = lax.rem(g + i, G)
-                gz_copy(ss.at[j], ss_in.at[j, frm], rs2_recv.at[j, frm], rs2_recv.at[j, frm], frm).wait_recv()
-            total = ss_in[j, 0].astype(F32)
+                gz_copy(ss.at[n], ss_in.at[n, frm], rs2_recv.at[n, frm], rs2_recv.at[n, frm], frm).wait_recv()
+            total = ss_in[n, 0].astype(F32)
             for i in range(1, G):
-                total = total + ss_in[j, i].astype(F32)
-            t32[j] = total
-            lax.fori_loop(0, NB_DEV, spread_back, 0)
+                total = total + ss_in[n, i].astype(F32)
+            for i in range(2):
+                b = 2 * k + i
+                wz = kz[b, :, BL * j:BL * (j + 1)]
+                wd = kzd[b, :, BL * j:BL * (j + 1)]
+                parts = []
+                for r in range(R):
+                    plain = total[4 * r + i:4 * r + i + 1]
+                    sloped = total[4 * r + 2 + i:4 * r + 3 + i]
+                    parts.append(jnp.concatenate([wz * plain + wd * sloped, wz * sloped], 1))
+                left = jnp.concatenate(parts, 0)
+                left_high = left.astype(BF16)
+                left_low = (left - left_high.astype(F32)).astype(BF16)
+                both = lax.dot_general(
+                    jnp.concatenate([left_high, left_low], 0),
+                    kt[b, :wide, 2 * BL * j:2 * BL * (j + 1)], NT, preferred_element_type=F32)
+                acc[:, :wide] += both[:R * SLAB] + both[R * SLAB:]
+
+        for k in range(PAIRS):
+            n = UNITS.index((k, j))
+
+            @pl.when(active(n, g))
+            def _(n=n, k=k, spread_back=spread_back):
+                spread_back(n, k)
 
         ordered = jnp.dot(order, acc[:, BL * j:BL * (j + 1)].astype(BF16), preferred_element_type=F32)
         bk[j] = ordered.astype(BF16).reshape(D, 16, BL)
@@ -333,16 +356,13 @@
         for k in range(3):
             back_out[k, :, BL * j:BL * (j + 1)] = total[4 * k:4 * k + 4]
 
-    for i in range(1, G):
-        to = lax.rem(g + i, G)
-        for j in range(BLOCKS):
-            @pl.when(active(j, g))
-            def _(i=i, j=j, to=to):
-                gz_copy(spb.at[j], sp_in.at[j, g], rs_send.at[j, i], rs_send.at[j, i], to).wait_send()
-
-            @pl.when(active(j, to))
-            def _(i=i, j=j, to=to):
-                gz_copy(ss.at[j], ss_in.at[j, g], rs2_send.at[j, i], rs2_send.at[j, i], to).wait_send()
+    for n in range(len(UNITS)):
+        @pl.when(active(n, g))
+        def _(n=n):
+            for i in range(1, G):
+                gz_copy(spb.at[n], sp_in.at[n, g], rs_send.at[n, i], rs_send.at[n, i], lax.rem(g + i, G)).wait_send()
+
+        each_slab(n, lambda copy: copy.wait_send())
     for i in range(1, D // 2):
         dom_copy(w_all.at[d], w_all.at[d], w_send.at[i], w_send.at[i], sib).wait_send()
     for i in range(0, D // 2):
@@ -374,13 +394,13 @@
             pltpu.VMEM((NB_DEV, SLAB, U), F32),
             pltpu.VMEM((NB_DEV, SLAB, U), F32),
             pltpu.VMEM((2 * NB_DEV, 128), F32),
+            pltpu.VMEM((len(UNITS), 16, BL), F32),
+            pltpu.VMEM((len(UNITS), 16, BL), BF16),
+            pltpu.VMEM((len(UNITS), G, 16, BL), BF16),
             pltpu.VMEM((BLOCKS, 64, BL), F32),
-            pltpu.VMEM((BLOCKS, 64, BL), BF16),
-            pltpu.VMEM((BLOCKS, G, 64, BL), BF16),
-            pltpu.VMEM((BLOCKS, 64, BL), F32),
-            pltpu.VMEM((BLOCKS, 64, BL), BF16),
-            pltpu.VMEM((BLOCKS, G, 64, BL), BF16),
-            pltpu.VMEM((BLOCKS, 64, BL), F32),
+            pltpu.VMEM((len(UNITS), 16, BL), F32),
+            pltpu.VMEM((len(UNITS), 16, BL), BF16),
+            pltpu.VMEM((len(UNITS), G, 16, BL), BF16),
             pltpu.VMEM((D, PART, WC + EXT), BF16),
             pltpu.VMEM((EXT, 2 * U), BF16),
             pltpu.VMEM((EXT, 2 * U), BF16),
@@ -389,7 +409,7 @@
             pltpu.VMEM((BLOCKS, D, 16, BL), BF16),
             pltpu.VMEM((1, ALLP), F32),
             pltpu.VMEM((D, 1, ALLP), F32),
-        ] + [dma((16,))] * 4 + [dma((BLOCKS, 16))] * 6 + [dma((16,))] * 2,
+        ] + [dma((16,))] * 4 + [dma((len(UNITS), 16))] * 4 + [dma((BLOCKS, 16))] * 2 + [dma((16,))] * 2,
         compiler_params=pltpu.CompilerParams(
             collective_id=0, has_side_effects=True, vmem_limit_bytes=60 << 20),
         name="tilt_refine",

time: 50.1 us -> 50.7 us (1.012)
  the two profiles are of different devices: /device:TPU:17 before, /device:TPU:1 now
where the time goes in v4:
time: 50.7 us; the launch traced here: 50.5 us
  Pallas kernels  47.4 us (93%)
  local copies, waits for them, and re-layouts  2.47 us (5%)
  between operations  0.65 us (1%)
    pallas_call x1, Pallas kernels, local(): pl.pallas_call(body, out_shape=(jax.ShapeDtypeStruct((1, PART), F32), jax...  47.4 us
    unnamed x4, local copies, waits for them, and re-layouts  2.47 us

profile of v4, /device:TPU:1, one launch (start us, length us, event | category | flops | bytes accessed | tf_op | source)
XLA Modules:
  0.0 50.5 jit_solution(10821343268294715213)
XLA Ops:
  0.6 47.4 %tilt_refine.1 = (f32[1,16]{1,0:T(1,128)}, f32[3,4,384]{2,1,0:T(4,128)}) custom-call(f32[48,4,384]{2,1,0:T(4,128)} %vol_hbm.1, bf16[16,4,384]{2,1,0:T(4,128)(2,1)} %obs_hbm.1, f32[32,2,384]{2,1,0:T(2,128)} %ctf_hbm.1, s32[16]{0:T(128)} %cls_hbm.1, s32[16]{0:T(128)} %bins_hbm.1), custom_call_target="tpu_custom_call" | custom-call | tf_op jit(solution)/shard_map/tilt_refine/pallas_call | solution.py:380
  48.0 0.0 copy-start
  48.0 0.6 %copy-done = f32[1,16]{1,0:T(1,128)S(1)} copy-done((f32[1,16]{1,0:T(1,128)S(1)}, f32[1,16]{1,0:T(1,128)}, u32[]{:S(2)}) %copy-start) | copy-done | bytes 88
  48.7 0.5 %copy.9 = f32[16]{0:T(128)} copy(f32[16]{0:T(128)S(1)} %bitcast.1) | data formatting | bytes 128
  49.2 1.3 %copy.10 = f32[3,4,384]{2,1,0:T(4,128)} copy(f32[3,4,384]{2,1,0:T(4,128)} %get-tuple-element.9) | data formatting | bytes 36864
Async XLA Ops:
  48.0 0.6 %copy-start = (f32[1,16]{1,0:T(1,128)S(1)}, f32[1,16]{1,0:T(1,128)}, u32[]{:S(2)}) copy-start(f32[1,16]{1,0:T(1,128)} %get-tuple-element.4) | copy-start | bytes 196

commit v5 on v4

--- a/solution.py
+++ b/solution.py
@@ -29,6 +29,7 @@
 UNITS = [(k, j) for j in range(BLOCKS) for k in range(PAIRS)]
 F32 = jnp.float32
 BF16 = jnp.bfloat16
+NU = len(UNITS)
 NT = (((1,), (1,)), ((), ()))
 
 
@@ -63,8 +64,16 @@
         device_id={"dom": to}, device_id_type=pl.DeviceIdType.MESH)
 
 
+def each(first, last, act):
+    def one(i, carry):
+        act(i)
+        return carry
+
+    lax.fori_loop(first, last, one, 0)
+
+
 def body(vol_hbm, obs_hbm, ctf_hbm, cls_hbm, bins_hbm, pose_out, back_out,
-         vol, obs, ctf, cls, bins, in_sem, vb, kt, kz, kzd, sc, sp, spb, sp_in, s_all, sf, ss, ss_in,
+         vol, obs, ctf, cls, bins, low, top, in_sem, vb, kt, kz, kzd, sc, sp, spb, sp_in, s_all, sf, ss, ss_in, rows_t,
          w_all, c2h, c2l, acc, bk, bk_in, pose_s, pose_in,
          w_send, w_recv, f_send, f_recv,
          rs_send, rs_recv, rs2_send, rs2_recv, b_send, b_recv, p_send, p_recv):
@@ -79,21 +88,18 @@
 
 
     barrier = pltpu.get_barrier_semaphore()
-    for i in range(1, D):
-        pl.semaphore_signal(barrier, inc=1, device_id={"dom": lax.rem(d + i, D)},
-                            device_id_type=pl.DeviceIdType.MESH)
-    for i in range(1, G):
-        pl.semaphore_signal(barrier, inc=1, device_id={"gz": lax.rem(g + i, G)},
-                            device_id_type=pl.DeviceIdType.MESH)
-
-    low, top = [], []
-    for row in slab_spans():
+    each(1, D, lambda i: pl.semaphore_signal(
+        barrier, inc=1, device_id={"dom": lax.rem(d + i, D)}, device_id_type=pl.DeviceIdType.MESH))
+    each(1, G, lambda i: pl.semaphore_signal(
+        barrier, inc=1, device_id={"gz": lax.rem(g + i, G)}, device_id_type=pl.DeviceIdType.MESH))
+
+    for n, row in enumerate(slab_spans()):
         least, most = jnp.int32(row[0][0]), jnp.int32(row[0][1])
         for k in range(1, D):
             least = jnp.where(d == k, row[k][0], least)
             most = jnp.where(d == k, row[k][1], most)
-        low.append(least)
-        top.append(most)
+        low[n] = least
+        top[n] = most
 
     def active(n, slab):
         return (low[n] <= slab) & (slab <= top[n])
@@ -150,8 +156,8 @@
         def extract(n, k, j=j, wide=wide, radius=radius, plane=plane, column=column):
             for i in range(2):
                 b = 2 * k + i
-                sine = sc[b:b + 1, :]
-                cosine = sc[NB_DEV + b:NB_DEV + b + 1, :]
+                sine = sc[pl.ds(b, 1), :]
+                cosine = sc[pl.ds(NB_DEV + b, 1), :]
                 tx = column - radius * cosine
                 fx = jnp.maximum(1.0 - tx * tx, 0.0)
                 kx = jnp.concatenate([fx * fx, (tx * fx) * (radius * sine * (-4.0 / U))], 1)
@@ -176,34 +182,37 @@
                         direct * wd + tilted * wz, axis=0, keepdims=True)
             spb[n] = sp[n].astype(BF16)
 
-        for k in range(PAIRS):
-            n = UNITS.index((k, j))
-
-            @pl.when(active(n, g))
-            def _(n=n, k=k, extract=extract):
-                extract(n, k)
+        def unit(k, j=j, extract=extract):
+            @pl.when(active(PAIRS * j + k, g))
+            def _():
+                extract(PAIRS * j + k, k)
+
+        each(0, PAIRS, unit)
 
     pl.semaphore_wait(barrier, (G - 1) + (D - 1))
 
-    for i in range(1, D // 2):
-        to = lax.rem(zpos + i, D // 2) * 2 + core
-        dom_copy(w_all.at[d], w_all.at[d], w_send.at[i], w_recv.at[d], to).start()
-    dom_copy(w_all.at[d], w_all.at[d], f_send.at[0], f_recv.at[d], sib).start()
-
-    for n in range(len(UNITS)):
+    each(1, D // 2, lambda i: dom_copy(
+        w_all.at[d], w_all.at[d], w_send, w_recv.at[d], lax.rem(zpos + i, D // 2) * 2 + core).start())
+    dom_copy(w_all.at[d], w_all.at[d], f_send, f_recv, sib).start()
+
+    def send_slices(n):
         @pl.when(active(n, g))
-        def _(n=n):
-            for i in range(1, G):
-                gz_copy(spb.at[n], sp_in.at[n, g], rs_send.at[n, i], rs_recv.at[n, g], lax.rem(g + i, G)).start()
+        def _():
+            each(1, G, lambda i: gz_copy(
+                spb.at[n], sp_in.at[n, g], rs_send.at[n], rs_recv.at[n, g], lax.rem(g + i, G)).start())
             sp_in[n, g] = spb[n]
 
-    for i in range(1, D // 2):
+    each(0, NU, send_slices)
+
+    def pass_on(i):
         frm = lax.rem(zpos + i, D // 2) * 2 + core
         dom_copy(w_all.at[frm], w_all.at[frm], w_recv.at[frm], w_recv.at[frm], sib).wait_recv()
-        dom_copy(w_all.at[frm], w_all.at[frm], f_send.at[i], f_recv.at[frm], sib).start()
-
-    for n, (k, j) in enumerate(UNITS):
-        def gather(frm, total, n=n):
+        dom_copy(w_all.at[frm], w_all.at[frm], f_send, f_recv, sib).start()
+
+    each(1, D // 2, pass_on)
+
+    def gather_slices(n):
+        def gather(frm, total):
             @pl.when(frm != g)
             def _():
                 gz_copy(spb.at[n], sp_in.at[n, frm], rs_recv.at[n, frm], rs_recv.at[n, frm],
@@ -211,8 +220,13 @@
             return total + sp_in[n, frm].astype(F32)
 
         total = lax.fori_loop(low[n], top[n] + 1, gather, jnp.zeros((16, BL), F32))
+        j = lax.div(n, PAIRS)
+        k = lax.rem(n, PAIRS)
         for m in range(8):
-            s_all[j, 8 * m + 2 * k:8 * m + 2 * k + 2, :] = total[2 * m:2 * m + 2]
+            for i in range(2):
+                s_all[j, pl.ds(8 * m + 2 * k + i, 1), :] = total[2 * m + i:2 * m + i + 1]
+
+    each(0, NU, gather_slices)
 
     def rows_of(kind, r):
         at = 32 * kind + 8 * r
@@ -237,9 +251,8 @@
     lookup = jnp.concatenate([tables_high, tables_low, pick, zero], 0)
     slope_rows = jnp.concatenate(slope, 1).astype(BF16)
 
-    for i in range(0, D // 2):
-        frm = lax.rem(zpos + i, D // 2) * 2 + 1 - core
-        dom_copy(w_all.at[frm], w_all.at[frm], f_recv.at[frm], f_recv.at[frm], sib).wait_recv()
+    half = w_all.at[0:D // 2]
+    dom_copy(half, half, f_recv, f_recv, sib).wait_recv()
 
     images = w_all[:, :, :WC].reshape(ALLP, WC)
     marks = w_all[:, :, WC:].reshape(ALLP, EXT)
@@ -271,19 +284,15 @@
     ss[...] = sf[...].astype(BF16)
 
     def each_slab(n, act):
-        def one(to, carry):
+        def one(to):
             @pl.when(to != g)
             def _():
-                act(gz_copy(ss.at[n], ss_in.at[n, g], rs2_send.at[n, to], rs2_recv.at[n, g], to))
-            return carry
-
-        lax.fori_loop(low[n], top[n] + 1, one, 0)
-
-    for n in reversed(range(len(UNITS))):
-        each_slab(n, lambda copy: copy.start())
-    for i in range(1, D):
-        to = lax.rem(d + i, D)
-        dom_copy(pose_s, pose_in.at[d], p_send.at[i], p_recv.at[d], to).start()
+                act(gz_copy(ss.at[n], ss_in.at[n, g], rs2_send.at[n, to], rs2_recv.at[n], to))
+
+        each(low[n], top[n] + 1, one)
+
+    each(0, NU, lambda n: each_slab(NU - 1 - n, lambda copy: copy.start()))
+    each(1, D, lambda i: dom_copy(pose_s, pose_in.at[d], p_send, p_recv, lax.rem(d + i, D)).start())
 
     acc[...] = jnp.zeros_like(acc)
     row = iota((256, R * SLAB), 0)
@@ -296,20 +305,17 @@
 
         def spread_back(n, k, j=j, wide=wide):
             ss_in[n, g] = ss[n]
-            for i in range(1, G):
-                frm = lax.rem(g + i, G)
-                gz_copy(ss.at[n], ss_in.at[n, frm], rs2_recv.at[n, frm], rs2_recv.at[n, frm], frm).wait_recv()
-            total = ss_in[n, 0].astype(F32)
-            for i in range(1, G):
-                total = total + ss_in[n, i].astype(F32)
+            others = ss_in.at[n, 0:G - 1]
+            gz_copy(others, others, rs2_recv.at[n], rs2_recv.at[n], lax.rem(g + 1, G)).wait_recv()
+            rows_t[...] = jnp.sum(ss_in[n].astype(F32), axis=0)
             for i in range(2):
                 b = 2 * k + i
                 wz = kz[b, :, BL * j:BL * (j + 1)]
                 wd = kzd[b, :, BL * j:BL * (j + 1)]
                 parts = []
                 for r in range(R):
-                    plain = total[4 * r + i:4 * r + i + 1]
-                    sloped = total[4 * r + 2 + i:4 * r + 3 + i]
+                    plain = rows_t[4 * r + i:4 * r + i + 1, :]
+                    sloped = rows_t[4 * r + 2 + i:4 * r + 3 + i, :]
                     parts.append(jnp.concatenate([wz * plain + wd * sloped, wz * sloped], 1))
                 left = jnp.concatenate(parts, 0)
                 left_high = left.astype(BF16)
@@ -319,26 +325,25 @@
                     kt[b, :wide, 2 * BL * j:2 * BL * (j + 1)], NT, preferred_element_type=F32)
                 acc[:, :wide] += both[:R * SLAB] + both[R * SLAB:]
 
-        for k in range(PAIRS):
-            n = UNITS.index((k, j))
-
-            @pl.when(active(n, g))
-            def _(n=n, k=k, spread_back=spread_back):
-                spread_back(n, k)
+        def unit(k, j=j, spread_back=spread_back):
+            @pl.when(active(PAIRS * j + k, g))
+            def _():
+                spread_back(PAIRS * j + k, k)
+
+        each(0, PAIRS, unit)
 
         ordered = jnp.dot(order, acc[:, BL * j:BL * (j + 1)].astype(BF16), preferred_element_type=F32)
         bk[j] = ordered.astype(BF16).reshape(D, 16, BL)
-        for i in range(1, D):
+        def send_block(i, j=j):
             to = lax.rem(d + i, D)
-            dom_copy(bk.at[j, to], bk_in.at[j, d], b_send.at[j, i], b_recv.at[j, d], to).start()
+            dom_copy(bk.at[j, to], bk_in.at[j, d], b_send.at[j], b_recv.at[j], to).start()
+
+        each(1, D, send_block)
 
     pose_in[d] = pose_s[...]
-    for i in range(1, D):
-        frm = lax.rem(d + i, D)
-        dom_copy(pose_s, pose_in.at[frm], p_recv.at[frm], p_recv.at[frm], frm).wait_recv()
-    pose = pose_in[0]
-    for i in range(1, D):
-        pose = pose + pose_in[i]
+    others = pose_in.at[0:D - 1]
+    dom_copy(others, others, p_recv, p_recv, sib).wait_recv()
+    pose = jnp.sum(pose_in[...], axis=0)
     lane = iota((8, ALLP), 1)
     kept = jnp.where(lax.div(lane, PART) == d, pose, 0.0)
     choose = (lax.rem(iota((ALLP, 128), 0), PART) == iota((ALLP, 128), 1)).astype(F32)
@@ -347,30 +352,29 @@
 
     for j in reversed(range(BLOCKS)):
         bk_in[j, d] = bk[j, d]
-        for i in range(1, D):
-            frm = lax.rem(d + i, D)
-            dom_copy(bk.at[j, 0], bk_in.at[j, frm], b_recv.at[j, frm], b_recv.at[j, frm], frm).wait_recv()
-        total = bk_in[j, 0].astype(F32)
-        for i in range(1, D):
-            total = total + bk_in[j, i].astype(F32)
+        others = bk_in.at[j, 0:D - 1]
+        dom_copy(others, others, b_recv.at[j], b_recv.at[j], sib).wait_recv()
+        total = jnp.sum(bk_in[j].astype(F32), axis=0)
         for k in range(3):
             back_out[k, :, BL * j:BL * (j + 1)] = total[4 * k:4 * k + 4]
 
-    for n in range(len(UNITS)):
+    def finish(n):
         @pl.when(active(n, g))
-        def _(n=n):
-            for i in range(1, G):
-                gz_copy(spb.at[n], sp_in.at[n, g], rs_send.at[n, i], rs_send.at[n, i], lax.rem(g + i, G)).wait_send()
+        def _():
+            sent = sp_in.at[n, 0:G - 1]
+            gz_copy(sent, sent, rs_send.at[n], rs_send.at[n], lax.rem(g + 1, G)).wait_send()
 
         each_slab(n, lambda copy: copy.wait_send())
-    for i in range(1, D // 2):
-        dom_copy(w_all.at[d], w_all.at[d], w_send.at[i], w_send.at[i], sib).wait_send()
-    for i in range(0, D // 2):
-        dom_copy(w_all.at[d], w_all.at[d], f_send.at[i], f_send.at[i], sib).wait_send()
-    for i in range(1, D):
-        for j in range(BLOCKS):
-            dom_copy(bk.at[j, 0], bk_in.at[j, d], b_send.at[j, i], b_send.at[j, i], sib).wait_send()
-        dom_copy(pose_s, pose_in.at[d], p_send.at[i], p_send.at[i], sib).wait_send()
+
+    each(0, NU, finish)
+    sent = w_all.at[0:D // 2 - 1]
+    dom_copy(sent, sent, w_send, w_send, sib).wait_send()
+    dom_copy(half, half, f_send, f_send, sib).wait_send()
+    sent = pose_in.at[0:D - 1]
+    dom_copy(sent, sent, p_send, p_send, sib).wait_send()
+    for j in range(BLOCKS):
+        sent = bk_in.at[j, 0:D - 1]
+        dom_copy(sent, sent, b_send.at[j], b_send.at[j], sib).wait_send()
 
 
 def local(volume, observed, ctf_table, ctf_class, bin_ids):
@@ -388,19 +392,22 @@
             pltpu.VMEM((NCTF, 2, U), F32),
             pltpu.SMEM((PART,), jnp.int32),
             pltpu.SMEM((PART,), jnp.int32),
+            pltpu.SMEM((NU,), jnp.int32),
+            pltpu.SMEM((NU,), jnp.int32),
             dma((5,)),
             pltpu.VMEM((2 * R * SLAB, X), BF16),
             pltpu.VMEM((NB_DEV, X, 2 * U), BF16),
             pltpu.VMEM((NB_DEV, SLAB, U), F32),
             pltpu.VMEM((NB_DEV, SLAB, U), F32),
             pltpu.VMEM((2 * NB_DEV, 128), F32),
-            pltpu.VMEM((len(UNITS), 16, BL), F32),
-            pltpu.VMEM((len(UNITS), 16, BL), BF16),
-            pltpu.VMEM((len(UNITS), G, 16, BL), BF16),
+            pltpu.VMEM((NU, 16, BL), F32),
+            pltpu.VMEM((NU, 16, BL), BF16),
+            pltpu.VMEM((NU, G, 16, BL), BF16),
             pltpu.VMEM((BLOCKS, 64, BL), F32),
-            pltpu.VMEM((len(UNITS), 16, BL), F32),
-            pltpu.VMEM((len(UNITS), 16, BL), BF16),
-            pltpu.VMEM((len(UNITS), G, 16, BL), BF16),
+            pltpu.VMEM((NU, 16, BL), F32),
+            pltpu.VMEM((NU, 16, BL), BF16),
+            pltpu.VMEM((NU, G, 16, BL), BF16),
+            pltpu.VMEM((16, BL), F32),
             pltpu.VMEM((D, PART, WC + EXT), BF16),
             pltpu.VMEM((EXT, 2 * U), BF16),
             pltpu.VMEM((EXT, 2 * U), BF16),
@@ -409,7 +416,11 @@
             pltpu.VMEM((BLOCKS, D, 16, BL), BF16),
             pltpu.VMEM((1, ALLP), F32),
             pltpu.VMEM((D, 1, ALLP), F32),
-        ] + [dma((16,))] * 4 + [dma((len(UNITS), 16))] * 4 + [dma((BLOCKS, 16))] * 2 + [dma((16,))] * 2,
+        ] + [
+            dma, dma((D,)), dma, dma,
+            dma((NU,)), dma((NU, G)), dma((NU, G)), dma((NU,)),
+            dma((BLOCKS,)), dma((BLOCKS,)), dma, dma,
+        ],
         compiler_params=pltpu.CompilerParams(
             collective_id=0, has_side_effects=True, vmem_limit_bytes=60 << 20),
         name="tilt_refine",

time: 50.7 us -> 46.1 us (0.909)
  Pallas kernels: 47.4 us -> 42.8 us
    pallas_call x1, Pallas kernels: 47.4 us -> 42.8 us  [local(): pl.pallas_call(body, out_shape=(jax.ShapeDtypeStruct((1, PART), F32), jax...]
where the time goes in v5:
time: 46.1 us; the launch traced here: 46 us
  Pallas kernels  42.8 us (93%)
  local copies, waits for them, and re-layouts  2.47 us (5%)
  between operations  0.65 us (1%)
    pallas_call x1, Pallas kernels, local(): pl.pallas_call(body, out_shape=(jax.ShapeDtypeStruct((1, PART), F32), jax...  42.8 us
    unnamed x4, local copies, waits for them, and re-layouts  2.47 us

profile of v5, /device:TPU:1, one launch (start us, length us, event | category | flops | bytes accessed | tf_op | source)
XLA Modules:
  0.0 46.0 jit_solution(6123845859884403413)
XLA Ops:
  0.6 42.8 %tilt_refine.1 = (f32[1,16]{1,0:T(1,128)}, f32[3,4,384]{2,1,0:T(4,128)}) custom-call(f32[48,4,384]{2,1,0:T(4,128)} %vol_hbm.1, bf16[16,4,384]{2,1,0:T(4,128)(2,1)} %obs_hbm.1, f32[32,2,384]{2,1,0:T(2,128)} %ctf_hbm.1, s32[16]{0:T(128)} %cls_hbm.1, s32[16]{0:T(128)} %bins_hbm.1), custom_call_target="tpu_custom_call" | custom-call | tf_op jit(solution)/shard_map/tilt_refine/pallas_call | solution.py:384
  43.5 0.0 copy-start
  43.5 0.6 %copy-done = f32[1,16]{1,0:T(1,128)S(1)} copy-done((f32[1,16]{1,0:T(1,128)S(1)}, f32[1,16]{1,0:T(1,128)}, u32[]{:S(2)}) %copy-start) | copy-done | bytes 88
  44.1 0.5 %copy.9 = f32[16]{0:T(128)} copy(f32[16]{0:T(128)S(1)} %bitcast.1) | data formatting | bytes 128
  44.6 1.3 %copy.10 = f32[3,4,384]{2,1,0:T(4,128)} copy(f32[3,4,384]{2,1,0:T(4,128)} %get-tuple-element.9) | data formatting | bytes 36864
Async XLA Ops:
  43.5 0.6 %copy-start = (f32[1,16]{1,0:T(1,128)S(1)}, f32[1,16]{1,0:T(1,128)}, u32[]{:S(2)}) copy-start(f32[1,16]{1,0:T(1,128)} %get-tuple-element.4) | copy-start | bytes 196

commit v6 on v5

--- a/solution.py
+++ b/solution.py
@@ -137,57 +137,57 @@
     c2l[:NCTF, :] = (square - high.astype(F32)).astype(BF16)
 
     fetches[4].wait()
-    for r in range(R):
-        plane_rows = vol[:, r, :]
-        coarse = plane_rows.astype(BF16)
-        vb[r * SLAB:(r + 1) * SLAB, :] = coarse
-        vb[(R + r) * SLAB:(R + r + 1) * SLAB, :] = (plane_rows - coarse.astype(F32)).astype(BF16)
+    def split_planes(part):
+        for r in range(R):
+            plane_rows = vol[pl.ds(16 * part, 16), r, :]
+            coarse = plane_rows.astype(BF16)
+            at = pl.multiple_of(r * SLAB + 16 * part, 16)
+            vb[pl.ds(at, 16), :] = coarse
+            vb[pl.ds(R * SLAB + at, 16), :] = (plane_rows - coarse.astype(F32)).astype(BF16)
+
+    each(0, SLAB // 16, split_planes)
     bin_index = bin_of(iota((NB_DEV, 128), 0)).astype(F32)
     theta = -0.5 * math.pi + math.pi * (bin_index + 0.5) / NB
     sc[:NB_DEV, :] = jnp.sin(theta)
     sc[NB_DEV:, :] = jnp.cos(theta)
-
-    for j in range(BLOCKS):
-        wide = BL * (j + 1)
+    plane = (g * SLAB + iota((SLAB, BL), 0)).astype(F32)
+    column = iota((X, BL), 0).astype(F32)
+
+    def extract(n, i):
+        j = lax.div(n, PAIRS)
+        b = 2 * lax.rem(n, PAIRS) + i
         radius = (BL * j + iota((1, BL), 1)).astype(F32)
-        plane = (g * SLAB + iota((SLAB, BL), 0)).astype(F32)
-        column = iota((wide, BL), 0).astype(F32)
-
-        def extract(n, k, j=j, wide=wide, radius=radius, plane=plane, column=column):
-            for i in range(2):
-                b = 2 * k + i
-                sine = sc[pl.ds(b, 1), :]
-                cosine = sc[pl.ds(NB_DEV + b, 1), :]
-                tx = column - radius * cosine
-                fx = jnp.maximum(1.0 - tx * tx, 0.0)
-                kx = jnp.concatenate([fx * fx, (tx * fx) * (radius * sine * (-4.0 / U))], 1)
-                kx_high = kx.astype(BF16)
-                kt[b, :wide, 2 * BL * j:2 * BL * (j + 1)] = kx_high
-                kx_low = (kx - kx_high.astype(F32)).astype(BF16)
-                tz = plane - (0.5 * NZ + radius * sine)
-                fz = jnp.maximum(1.0 - tz * tz, 0.0)
-                wz = fz * fz
-                wd = (tz * fz) * (radius * cosine * (4.0 / U))
-                kz[b, :, BL * j:BL * (j + 1)] = wz
-                kzd[b, :, BL * j:BL * (j + 1)] = wd
-                stacked = jnp.dot(vb[:, :wide], kx_high, preferred_element_type=F32)
-                both = stacked[:R * SLAB] + stacked[R * SLAB:] + jnp.dot(
-                    vb[:R * SLAB, :wide], kx_low, preferred_element_type=F32)
-                for r in range(R):
-                    direct = both[r * SLAB:(r + 1) * SLAB, :BL]
-                    tilted = both[r * SLAB:(r + 1) * SLAB, BL:]
-                    at = 2 * r + i
-                    sp[n, at:at + 1, :] = jnp.sum(direct * wz, axis=0, keepdims=True)
-                    sp[n, 8 + at:8 + at + 1, :] = jnp.sum(
-                        direct * wd + tilted * wz, axis=0, keepdims=True)
+        sine = sc[pl.ds(b, 1), :]
+        cosine = sc[pl.ds(NB_DEV + b, 1), :]
+        tx = column - radius * cosine
+        fx = jnp.maximum(1.0 - tx * tx, 0.0)
+        kx = jnp.concatenate([fx * fx, (tx * fx) * (radius * sine * (-4.0 / U))], 1)
+        kx_high = kx.astype(BF16)
+        kt[n, i] = kx_high
+        kx_low = (kx - kx_high.astype(F32)).astype(BF16)
+        tz = plane - (0.5 * NZ + radius * sine)
+        fz = jnp.maximum(1.0 - tz * tz, 0.0)
+        wz = fz * fz
+        wd = (tz * fz) * (radius * cosine * (4.0 / U))
+        kz[n, i] = wz
+        kzd[n, i] = wd
+        stacked = jnp.dot(vb[...], kx_high, preferred_element_type=F32)
+        both = stacked[:R * SLAB] + stacked[R * SLAB:] + jnp.dot(
+            vb[:R * SLAB, :], kx_low, preferred_element_type=F32)
+        for r in range(R):
+            direct = both[r * SLAB:(r + 1) * SLAB, :BL]
+            tilted = both[r * SLAB:(r + 1) * SLAB, BL:]
+            sp[n, pl.ds(2 * r + i, 1), :] = jnp.sum(direct * wz, axis=0, keepdims=True)
+            sp[n, pl.ds(8 + 2 * r + i, 1), :] = jnp.sum(
+                direct * wd + tilted * wz, axis=0, keepdims=True)
+
+    def extract_unit(n):
+        @pl.when(active(n, g))
+        def _():
+            each(0, 2, lambda i: extract(n, i))
             spb[n] = sp[n].astype(BF16)
 
-        def unit(k, j=j, extract=extract):
-            @pl.when(active(PAIRS * j + k, g))
-            def _():
-                extract(PAIRS * j + k, k)
-
-        each(0, PAIRS, unit)
+    each(0, NU, extract_unit)
 
     pl.semaphore_wait(barrier, (G - 1) + (D - 1))
 
@@ -300,45 +300,47 @@
     source = lax.rem(row, 4) * SLAB + 3 * lax.div(row, 16) + lax.div(within, 4)
     order = ((iota((256, R * SLAB), 1) == source) & (within < 12)).astype(F32).astype(BF16)
 
-    for j in reversed(range(BLOCKS)):
-        wide = BL * (j + 1)
-
-        def spread_back(n, k, j=j, wide=wide):
+    def spread_back(n, i):
+        wz = kz[n, i]
+        wd = kzd[n, i]
+        parts = []
+        for r in range(R):
+            plain = rows_t[pl.ds(4 * r + i, 1), :]
+            sloped = rows_t[pl.ds(4 * r + 2 + i, 1), :]
+            parts.append(jnp.concatenate([wz * plain + wd * sloped, wz * sloped], 1))
+        left = jnp.concatenate(parts, 0)
+        left_high = left.astype(BF16)
+        left_low = (left - left_high.astype(F32)).astype(BF16)
+        both = lax.dot_general(
+            jnp.concatenate([left_high, left_low], 0), kt[n, i], NT, preferred_element_type=F32)
+        acc[...] += both[:R * SLAB] + both[R * SLAB:]
+
+    def spread_unit(n):
+        @pl.when(active(n, g))
+        def _():
             ss_in[n, g] = ss[n]
             others = ss_in.at[n, 0:G - 1]
             gz_copy(others, others, rs2_recv.at[n], rs2_recv.at[n], lax.rem(g + 1, G)).wait_recv()
             rows_t[...] = jnp.sum(ss_in[n].astype(F32), axis=0)
-            for i in range(2):
-                b = 2 * k + i
-                wz = kz[b, :, BL * j:BL * (j + 1)]
-                wd = kzd[b, :, BL * j:BL * (j + 1)]
-                parts = []
-                for r in range(R):
-                    plain = rows_t[4 * r + i:4 * r + i + 1, :]
-                    sloped = rows_t[4 * r + 2 + i:4 * r + 3 + i, :]
-                    parts.append(jnp.concatenate([wz * plain + wd * sloped, wz * sloped], 1))
-                left = jnp.concatenate(parts, 0)
-                left_high = left.astype(BF16)
-                left_low = (left - left_high.astype(F32)).astype(BF16)
-                both = lax.dot_general(
-                    jnp.concatenate([left_high, left_low], 0),
-                    kt[b, :wide, 2 * BL * j:2 * BL * (j + 1)], NT, preferred_element_type=F32)
-                acc[:, :wide] += both[:R * SLAB] + both[R * SLAB:]
-
-        def unit(k, j=j, spread_back=spread_back):
-            @pl.when(active(PAIRS * j + k, g))
-            def _():
-                spread_back(PAIRS * j + k, k)
-
-        each(0, PAIRS, unit)
-
-        ordered = jnp.dot(order, acc[:, BL * j:BL * (j + 1)].astype(BF16), preferred_element_type=F32)
+            each(0, 2, lambda i: spread_back(n, i))
+
+    def send_block(j):
+        at = pl.ds(pl.multiple_of(BL * j, BL), BL)
+        ordered = jnp.dot(order, acc[:, at].astype(BF16), preferred_element_type=F32)
         bk[j] = ordered.astype(BF16).reshape(D, 16, BL)
-        def send_block(i, j=j):
+
+        def send(i):
             to = lax.rem(d + i, D)
             dom_copy(bk.at[j, to], bk_in.at[j, d], b_send.at[j], b_recv.at[j], to).start()
 
-        each(1, D, send_block)
+        each(1, D, send)
+
+    def finish_block(back):
+        j = BLOCKS - 1 - back
+        each(0, PAIRS, lambda k: spread_unit(PAIRS * j + k))
+        send_block(j)
+
+    each(0, BLOCKS, finish_block)
 
     pose_in[d] = pose_s[...]
     others = pose_in.at[0:D - 1]
@@ -396,9 +398,9 @@
             pltpu.SMEM((NU,), jnp.int32),
             dma((5,)),
             pltpu.VMEM((2 * R * SLAB, X), BF16),
-            pltpu.VMEM((NB_DEV, X, 2 * U), BF16),
-            pltpu.VMEM((NB_DEV, SLAB, U), F32),
-            pltpu.VMEM((NB_DEV, SLAB, U), F32),
+            pltpu.VMEM((NU, 2, X, 2 * BL), BF16),
+            pltpu.VMEM((NU, 2, SLAB, BL), F32),
+            pltpu.VMEM((NU, 2, SLAB, BL), F32),
             pltpu.VMEM((2 * NB_DEV, 128), F32),
             pltpu.VMEM((NU, 16, BL), F32),
             pltpu.VMEM((NU, 16, BL), BF16),

time: 46.1 us -> 47.4 us (1.028)
  Pallas kernels: 42.8 us -> 44.1 us
    pallas_call x1, Pallas kernels: 42.8 us -> 44.1 us  [local(): pl.pallas_call(body, out_shape=(jax.ShapeDtypeStruct((1, PART), F32), jax...]
where the time goes in v6:
time: 47.4 us; the launch traced here: 47.2 us
  Pallas kernels  44.1 us (93%)
  local copies, waits for them, and re-layouts  2.47 us (5%)
  between operations  0.65 us (1%)
    pallas_call x1, Pallas kernels, local(): pl.pallas_call(body, out_shape=(jax.ShapeDtypeStruct((1, PART), F32), jax...  44.1 us
    unnamed x4, local copies, waits for them, and re-layouts  2.47 us

profile of v6, /device:TPU:1, one launch (start us, length us, event | category | flops | bytes accessed | tf_op | source)
XLA Modules:
  0.0 47.2 jit_solution(2794173866221241808)
XLA Ops:
  0.6 44.1 %tilt_refine.1 = (f32[1,16]{1,0:T(1,128)}, f32[3,4,384]{2,1,0:T(4,128)}) custom-call(f32[48,4,384]{2,1,0:T(4,128)} %vol_hbm.1, bf16[16,4,384]{2,1,0:T(4,128)(2,1)} %obs_hbm.1, f32[32,2,384]{2,1,0:T(2,128)} %ctf_hbm.1, s32[16]{0:T(128)} %cls_hbm.1, s32[16]{0:T(128)} %bins_hbm.1), custom_call_target="tpu_custom_call" | custom-call | tf_op jit(solution)/shard_map/tilt_refine/pallas_call | solution.py:386
  44.8 0.0 copy-start
  44.8 0.6 %copy-done = f32[1,16]{1,0:T(1,128)S(1)} copy-done((f32[1,16]{1,0:T(1,128)S(1)}, f32[1,16]{1,0:T(1,128)}, u32[]{:S(2)}) %copy-start) | copy-done | bytes 88
  45.4 0.5 %copy.9 = f32[16]{0:T(128)} copy(f32[16]{0:T(128)S(1)} %bitcast.1) | data formatting | bytes 128
  45.9 1.3 %copy.10 = f32[3,4,384]{2,1,0:T(4,128)} copy(f32[3,4,384]{2,1,0:T(4,128)} %get-tuple-element.9) | data formatting | bytes 36864
Async XLA Ops:
  44.8 0.6 %copy-start = (f32[1,16]{1,0:T(1,128)S(1)}, f32[1,16]{1,0:T(1,128)}, u32[]{:S(2)}) copy-start(f32[1,16]{1,0:T(1,128)} %get-tuple-element.4) | copy-start | bytes 196

commit v7 on v5

--- a/solution.py
+++ b/solution.py
@@ -75,7 +75,7 @@
 def body(vol_hbm, obs_hbm, ctf_hbm, cls_hbm, bins_hbm, pose_out, back_out,
          vol, obs, ctf, cls, bins, low, top, in_sem, vb, kt, kz, kzd, sc, sp, spb, sp_in, s_all, sf, ss, ss_in, rows_t,
          w_all, c2h, c2l, acc, bk, bk_in, pose_s, pose_in,
-         w_send, w_recv, f_send, f_recv,
+         ids, ids_in, w_send, w_recv, f_send, f_recv, i_send, i_recv,
          rs_send, rs_recv, rs2_send, rs2_recv, b_send, b_recv, p_send, p_recv):
     g = lax.axis_index("gz")
     d = lax.axis_index("dom")
@@ -111,23 +111,29 @@
     for fetch in fetches[:4]:
         fetch.wait()
 
-    rows = iota((PART, EXT), 0)
-    lanes = iota((PART, EXT), 1)
-    cls_col = jnp.zeros((PART, EXT), jnp.int32)
-    bin_col = jnp.zeros((PART, EXT), jnp.int32)
+    rows = iota((PART, NCTF), 0)
+    along_row = iota((1, ALLP), 1) - PART * d
+    cls_col = jnp.zeros((PART, NCTF), jnp.int32)
+    id_row = jnp.zeros((1, ALLP), jnp.int32)
     for i in range(PART):
         cls_col = jnp.where(rows == i, cls[i], cls_col)
-        bin_col = jnp.where(rows == i, bins[i], bin_col)
-    cls_hot = (cls_col == lanes).astype(F32)
+        id_row = jnp.where(along_row == i, NCTF * bins[i] + cls[i], id_row)
+    cls_hot = (cls_col == iota((PART, NCTF), 1)).astype(F32)
+    ids[...] = id_row.astype(F32)
     table = jnp.concatenate([ctf[:, 0, :], ctf[:, 1, :]], 1)
-    contrast = jnp.dot(cls_hot[:, :NCTF], table, precision=lax.Precision.HIGHEST,
+    contrast = jnp.dot(cls_hot, table, precision=lax.Precision.HIGHEST,
                        preferred_element_type=F32)
     for r in range(R):
         y = r % 2
         image = obs[:, r, :].astype(F32)
         w_all[d, :, r * U:(r + 1) * U] = (image * contrast[:, y * U:(y + 1) * U]).astype(BF16)
-    extra = jnp.where(lanes == NCTF, bin_col.astype(F32), cls_hot)
-    w_all[d, :, WC:] = extra.astype(BF16)
+
+    pl.semaphore_wait(barrier, (G - 1) + (D - 1))
+
+    each(1, D // 2, lambda i: dom_copy(
+        w_all.at[d], w_all.at[d], w_send, w_recv.at[d], lax.rem(zpos + i, D // 2) * 2 + core).start())
+    dom_copy(w_all.at[d], w_all.at[d], f_send, f_recv, sib).start()
+    each(1, D, lambda i: dom_copy(ids, ids_in.at[d], i_send, i_recv, lax.rem(d + i, D)).start())
 
     square = table * table
     high = square.astype(BF16)
@@ -137,11 +143,15 @@
     c2l[:NCTF, :] = (square - high.astype(F32)).astype(BF16)
 
     fetches[4].wait()
-    for r in range(R):
-        plane_rows = vol[:, r, :]
-        coarse = plane_rows.astype(BF16)
-        vb[r * SLAB:(r + 1) * SLAB, :] = coarse
-        vb[(R + r) * SLAB:(R + r + 1) * SLAB, :] = (plane_rows - coarse.astype(F32)).astype(BF16)
+    def split_planes(part):
+        for r in range(R):
+            plane_rows = vol[pl.ds(16 * part, 16), r, :]
+            coarse = plane_rows.astype(BF16)
+            at = pl.multiple_of(r * SLAB + 16 * part, 16)
+            vb[pl.ds(at, 16), :] = coarse
+            vb[pl.ds(R * SLAB + at, 16), :] = (plane_rows - coarse.astype(F32)).astype(BF16)
+
+    each(0, SLAB // 16, split_planes)
     bin_index = bin_of(iota((NB_DEV, 128), 0)).astype(F32)
     theta = -0.5 * math.pi + math.pi * (bin_index + 0.5) / NB
     sc[:NB_DEV, :] = jnp.sin(theta)
@@ -189,12 +199,6 @@
 
         each(0, PAIRS, unit)
 
-    pl.semaphore_wait(barrier, (G - 1) + (D - 1))
-
-    each(1, D // 2, lambda i: dom_copy(
-        w_all.at[d], w_all.at[d], w_send, w_recv.at[d], lax.rem(zpos + i, D // 2) * 2 + core).start())
-    dom_copy(w_all.at[d], w_all.at[d], f_send, f_recv, sib).start()
-
     def send_slices(n):
         @pl.when(active(n, g))
         def _():
@@ -203,13 +207,6 @@
             sp_in[n, g] = spb[n]
 
     each(0, NU, send_slices)
-
-    def pass_on(i):
-        frm = lax.rem(zpos + i, D // 2) * 2 + core
-        dom_copy(w_all.at[frm], w_all.at[frm], w_recv.at[frm], w_recv.at[frm], sib).wait_recv()
-        dom_copy(w_all.at[frm], w_all.at[frm], f_send, f_recv, sib).start()
-
-    each(1, D // 2, pass_on)
 
     def gather_slices(n):
         def gather(frm, total):
@@ -246,41 +243,52 @@
                                                        preferred_element_type=F32)
     tables_high = tables.astype(BF16)
     tables_low = (tables - tables_high.astype(F32)).astype(BF16)
-    pick = (iota((8, EXT), 1) == NCTF).astype(F32).astype(BF16)
-    zero = jnp.zeros((8, EXT), BF16)
-    lookup = jnp.concatenate([tables_high, tables_low, pick, zero], 0)
+    lookup = jnp.concatenate([tables_high, tables_low], 0)[:, :NCTF]
     slope_rows = jnp.concatenate(slope, 1).astype(BF16)
 
+    ids_in[d] = ids[...]
+    others = ids_in.at[0:D - 1]
+    dom_copy(others, others, i_recv, i_recv, sib).wait_recv()
+    id_row = jnp.sum(ids_in[...], axis=0).astype(jnp.int32)
+    bin_row = lax.div(id_row, NCTF)
+    cls_rows = (iota((NCTF, ALLP), 0) == lax.rem(id_row, NCTF)).astype(F32).astype(BF16)
+    looked = jnp.dot(lookup, cls_rows, preferred_element_type=F32)
+    held = looked[0:8] + looked[16:24]
+    crossed = looked[8:16] + looked[24:32]
+    mask = (bin_of(iota((8, ALLP), 0)) == bin_row).astype(F32)
+    power = jnp.sum(mask * held, axis=0, keepdims=True)
+    cross_row = jnp.sum(mask * crossed, axis=0, keepdims=True)
+    curvature = power + EPS
+    slot = iota((16, ALLP), 0)
+    sloped_row = lax.rem(lax.div(slot, 2), 2) == 1
+    mask_rows = (2 * d + 2 * D * lax.div(slot, 4) + lax.rem(slot, 2) == bin_row).astype(F32)
+
+    def pass_on(i):
+        step = lax.div(i + 1, 2) * (1 - 2 * lax.rem(i, 2))
+        frm = lax.rem(zpos + step + D // 2, D // 2) * 2 + core
+        dom_copy(w_all.at[frm], w_all.at[frm], w_recv.at[frm], w_recv.at[frm], sib).wait_recv()
+        dom_copy(w_all.at[frm], w_all.at[frm], f_send, f_recv, sib).start()
+
+    each(1, D // 2, pass_on)
     half = w_all.at[0:D // 2]
     dom_copy(half, half, f_recv, f_recv, sib).wait_recv()
 
-    images = w_all[:, :, :WC].reshape(ALLP, WC)
-    marks = w_all[:, :, WC:].reshape(ALLP, EXT)
-    looked = lax.dot_general(lookup, marks, NT, preferred_element_type=F32)
+    images = w_all[...].reshape(ALLP, WC)
     along = lax.dot_general(slope_rows, images, NT, preferred_element_type=F32)
-    held = looked[0:8] + looked[16:24]
-    crossed = looked[8:16] + looked[24:32]
-    own = bin_of(iota((8, ALLP), 0)).astype(F32) == looked[32:40]
-    mask = own.astype(F32)
-    power = jnp.sum(mask * held, axis=0, keepdims=True)
-    match = jnp.sum(mask * (along - crossed), axis=0, keepdims=True)
-    curvature = power + EPS
+    match = jnp.sum(mask * along, axis=0, keepdims=True) - cross_row
     shift = jnp.zeros_like(power)
     for _ in range(ITERS):
         shift = shift + 0.5 * (match - shift * power) / curvature
     pose_s[...] = shift * jnp.sqrt(curvature)
-    moved = mask * shift
-    moved_high = moved.astype(BF16)
-    moved_low = (moved - moved_high.astype(F32)).astype(BF16)
-    spread = jnp.concatenate([mask.astype(BF16), moved_high, moved_low, jnp.zeros((8, ALLP), BF16)], 0)
-    sums = jnp.dot(spread, images, preferred_element_type=F32)
-    for r in range(R):
-        part = sums[:, r * U:(r + 1) * U]
-        plain = part[:8]
-        sloped = part[8:16] + part[16:24]
-        for n, (k, j) in enumerate(UNITS):
-            sf[n, 4 * r:4 * r + 2, :] = plain[2 * k:2 * k + 2, BL * j:BL * (j + 1)]
-            sf[n, 4 * r + 2:4 * r + 4, :] = sloped[2 * k:2 * k + 2, BL * j:BL * (j + 1)]
+    spread = mask_rows * jnp.where(sloped_row, shift, 1.0)
+    spread_high = spread.astype(BF16)
+    spread_low = (spread - spread_high.astype(F32)).astype(BF16)
+    sums = jnp.dot(jnp.concatenate([spread_high, spread_low], 0), images, preferred_element_type=F32)
+    sums = sums[:16] + sums[16:]
+    for n, (k, j) in enumerate(UNITS):
+        for r in range(R):
+            at = r * U + BL * j
+            sf[n, 4 * r:4 * r + 4, :] = sums[4 * k:4 * k + 4, at:at + BL]
     ss[...] = sf[...].astype(BF16)
 
     def each_slab(n, act):
@@ -350,6 +358,23 @@
     picked = jnp.dot(kept, choose, precision=lax.Precision.HIGHEST, preferred_element_type=F32)
     pose_out[...] = picked[0:1, :PART]
 
+    def finish(n):
+        @pl.when(active(n, g))
+        def _():
+            sent = sp_in.at[n, 0:G - 1]
+            gz_copy(sent, sent, rs_send.at[n], rs_send.at[n], lax.rem(g + 1, G)).wait_send()
+
+        each_slab(n, lambda copy: copy.wait_send())
+
+    each(0, NU, finish)
+    sent = w_all.at[0:D // 2 - 1]
+    dom_copy(sent, sent, w_send, w_send, sib).wait_send()
+    dom_copy(half, half, f_send, f_send, sib).wait_send()
+    sent = pose_in.at[0:D - 1]
+    dom_copy(sent, sent, p_send, p_send, sib).wait_send()
+    sent = ids_in.at[0:D - 1]
+    dom_copy(sent, sent, i_send, i_send, sib).wait_send()
+
     for j in reversed(range(BLOCKS)):
         bk_in[j, d] = bk[j, d]
         others = bk_in.at[j, 0:D - 1]
@@ -358,20 +383,6 @@
         for k in range(3):
             back_out[k, :, BL * j:BL * (j + 1)] = total[4 * k:4 * k + 4]
 
-    def finish(n):
-        @pl.when(active(n, g))
-        def _():
-            sent = sp_in.at[n, 0:G - 1]
-            gz_copy(sent, sent, rs_send.at[n], rs_send.at[n], lax.rem(g + 1, G)).wait_send()
-
-        each_slab(n, lambda copy: copy.wait_send())
-
-    each(0, NU, finish)
-    sent = w_all.at[0:D // 2 - 1]
-    dom_copy(sent, sent, w_send, w_send, sib).wait_send()
-    dom_copy(half, half, f_send, f_send, sib).wait_send()
-    sent = pose_in.at[0:D - 1]
-    dom_copy(sent, sent, p_send, p_send, sib).wait_send()
     for j in range(BLOCKS):
         sent = bk_in.at[j, 0:D - 1]
         dom_copy(sent, sent, b_send.at[j], b_send.at[j], sib).wait_send()
@@ -408,7 +419,7 @@
             pltpu.VMEM((NU, 16, BL), BF16),
             pltpu.VMEM((NU, G, 16, BL), BF16),
             pltpu.VMEM((16, BL), F32),
-            pltpu.VMEM((D, PART, WC + EXT), BF16),
+            pltpu.VMEM((D, PART, WC), BF16),
             pltpu.VMEM((EXT, 2 * U), BF16),
             pltpu.VMEM((EXT, 2 * U), BF16),
             pltpu.VMEM((R * SLAB, X), F32),
@@ -417,7 +428,9 @@
             pltpu.VMEM((1, ALLP), F32),
             pltpu.VMEM((D, 1, ALLP), F32),
         ] + [
-            dma, dma((D,)), dma, dma,
+            pltpu.VMEM((1, ALLP), F32),
+            pltpu.VMEM((D, 1, ALLP), F32),
+            dma, dma((D,)), dma, dma, dma, dma,
             dma((NU,)), dma((NU, G)), dma((NU, G)), dma((NU,)),
             dma((BLOCKS,)), dma((BLOCKS,)), dma, dma,
         ],

time: 46.1 us -> 45.8 us (level)
  no operation moved by 1% of the time
where the time goes in v7:
time: 45.8 us; the launch traced here: 45.7 us
  Pallas kernels  42.6 us (93%)
  local copies, waits for them, and re-layouts  2.47 us (5%)
  between operations  0.65 us (1%)
    pallas_call x1, Pallas kernels, local(): pl.pallas_call(body, out_shape=(jax.ShapeDtypeStruct((1, PART), F32), jax...  42.6 us
    unnamed x4, local copies, waits for them, and re-layouts  2.47 us

profile of v7, /device:TPU:1, one launch (start us, length us, event | category | flops | bytes accessed | tf_op | source)
XLA Modules:
  0.0 45.7 jit_solution(3717583291945535229)
XLA Ops:
  0.6 42.6 %tilt_refine.1 = (f32[1,16]{1,0:T(1,128)}, f32[3,4,384]{2,1,0:T(4,128)}) custom-call(f32[48,4,384]{2,1,0:T(4,128)} %vol_hbm.1, bf16[16,4,384]{2,1,0:T(4,128)(2,1)} %obs_hbm.1, f32[32,2,384]{2,1,0:T(2,128)} %ctf_hbm.1, s32[16]{0:T(128)} %cls_hbm.1, s32[16]{0:T(128)} %bins_hbm.1), custom_call_target="tpu_custom_call" | custom-call | tf_op jit(solution)/shard_map/tilt_refine/pallas_call | solution.py:395
  43.2 0.0 copy-start
  43.2 0.6 %copy-done = f32[1,16]{1,0:T(1,128)S(1)} copy-done((f32[1,16]{1,0:T(1,128)S(1)}, f32[1,16]{1,0:T(1,128)}, u32[]{:S(2)}) %copy-start) | copy-done | bytes 88
  43.8 0.5 %copy.9 = f32[16]{0:T(128)} copy(f32[16]{0:T(128)S(1)} %bitcast.1) | data formatting | bytes 128
  44.4 1.3 %copy.10 = f32[3,4,384]{2,1,0:T(4,128)} copy(f32[3,4,384]{2,1,0:T(4,128)} %get-tuple-element.9) | data formatting | bytes 36864
Async XLA Ops:
  43.2 0.6 %copy-start = (f32[1,16]{1,0:T(1,128)S(1)}, f32[1,16]{1,0:T(1,128)}, u32[]{:S(2)}) copy-start(f32[1,16]{1,0:T(1,128)} %get-tuple-element.4) | copy-start | bytes 196

commit v8 on v7

--- a/solution.py
+++ b/solution.py
@@ -72,8 +72,12 @@
     lax.fori_loop(first, last, one, 0)
 
 
-def body(vol_hbm, obs_hbm, ctf_hbm, cls_hbm, bins_hbm, pose_out, back_out,
-         vol, obs, ctf, cls, bins, low, top, in_sem, vb, kt, kz, kzd, sc, sp, spb, sp_in, s_all, sf, ss, ss_in, rows_t,
+def far_first(i, n):
+    return n // 2 + lax.div(i, 2) * (2 * lax.rem(i, 2) - 1)
+
+
+def body(vol_hbm, obs_hbm, ctf_hbm, mark_hbm, pose_out, back_out,
+         vol, obs, ctf, mark, low, top, in_sem, vb, kt, kz, kzd, sc, sp, spb, sp_in, s_all, sf, ss, ss_in, rows_t,
          w_all, c2h, c2l, acc, bk, bk_in, pose_s, pose_in,
          ids, ids_in, w_send, w_recv, f_send, f_recv, i_send, i_recv,
          rs_send, rs_recv, rs2_send, rs2_recv, b_send, b_recv, p_send, p_recv):
@@ -105,10 +109,10 @@
         return (low[n] <= slab) & (slab <= top[n])
 
     fetches = [pltpu.make_async_copy(src, dst, in_sem.at[k]) for k, (src, dst) in enumerate(
-        ((bins_hbm, bins), (cls_hbm, cls), (obs_hbm, obs), (ctf_hbm, ctf), (vol_hbm, vol)))]
+        ((mark_hbm, mark), (obs_hbm, obs), (ctf_hbm, ctf), (vol_hbm, vol)))]
     for fetch in fetches:
         fetch.start()
-    for fetch in fetches[:4]:
+    for fetch in fetches[:3]:
         fetch.wait()
 
     rows = iota((PART, NCTF), 0)
@@ -116,8 +120,8 @@
     cls_col = jnp.zeros((PART, NCTF), jnp.int32)
     id_row = jnp.zeros((1, ALLP), jnp.int32)
     for i in range(PART):
-        cls_col = jnp.where(rows == i, cls[i], cls_col)
-        id_row = jnp.where(along_row == i, NCTF * bins[i] + cls[i], id_row)
+        cls_col = jnp.where(rows == i, lax.rem(mark[i], NCTF), cls_col)
+        id_row = jnp.where(along_row == i, mark[i], id_row)
     cls_hot = (cls_col == iota((PART, NCTF), 1)).astype(F32)
     ids[...] = id_row.astype(F32)
     table = jnp.concatenate([ctf[:, 0, :], ctf[:, 1, :]], 1)
@@ -131,7 +135,7 @@
     pl.semaphore_wait(barrier, (G - 1) + (D - 1))
 
     each(1, D // 2, lambda i: dom_copy(
-        w_all.at[d], w_all.at[d], w_send, w_recv.at[d], lax.rem(zpos + i, D // 2) * 2 + core).start())
+        w_all.at[d], w_all.at[d], w_send, w_recv.at[d], lax.rem(zpos + far_first(i, D // 2), D // 2) * 2 + core).start())
     dom_copy(w_all.at[d], w_all.at[d], f_send, f_recv, sib).start()
     each(1, D, lambda i: dom_copy(ids, ids_in.at[d], i_send, i_recv, lax.rem(d + i, D)).start())
 
@@ -142,7 +146,7 @@
     c2h[:NCTF, :] = high
     c2l[:NCTF, :] = (square - high.astype(F32)).astype(BF16)
 
-    fetches[4].wait()
+    fetches[3].wait()
     def split_planes(part):
         for r in range(R):
             plane_rows = vol[pl.ds(16 * part, 16), r, :]
@@ -208,6 +212,12 @@
 
     each(0, NU, send_slices)
 
+    def pass_on(i):
+        frm = lax.rem(zpos + far_first(i, D // 2), D // 2) * 2 + core
+        dom_copy(w_all.at[frm], w_all.at[frm], w_recv.at[frm], w_recv.at[frm], sib).wait_recv()
+        dom_copy(w_all.at[frm], w_all.at[frm], f_send, f_recv, sib).start()
+
+    each(1, D // 2, pass_on)
     def gather_slices(n):
         def gather(frm, total):
             @pl.when(frm != g)
@@ -263,13 +273,6 @@
     sloped_row = lax.rem(lax.div(slot, 2), 2) == 1
     mask_rows = (2 * d + 2 * D * lax.div(slot, 4) + lax.rem(slot, 2) == bin_row).astype(F32)
 
-    def pass_on(i):
-        step = lax.div(i + 1, 2) * (1 - 2 * lax.rem(i, 2))
-        frm = lax.rem(zpos + step + D // 2, D // 2) * 2 + core
-        dom_copy(w_all.at[frm], w_all.at[frm], w_recv.at[frm], w_recv.at[frm], sib).wait_recv()
-        dom_copy(w_all.at[frm], w_all.at[frm], f_send, f_recv, sib).start()
-
-    each(1, D // 2, pass_on)
     half = w_all.at[0:D // 2]
     dom_copy(half, half, f_recv, f_recv, sib).wait_recv()
 
@@ -343,7 +346,7 @@
         ordered = jnp.dot(order, acc[:, BL * j:BL * (j + 1)].astype(BF16), preferred_element_type=F32)
         bk[j] = ordered.astype(BF16).reshape(D, 16, BL)
         def send_block(i, j=j):
-            to = lax.rem(d + i, D)
+            to = lax.rem(d + far_first(i, D), D)
             dom_copy(bk.at[j, to], bk_in.at[j, d], b_send.at[j], b_recv.at[j], to).start()
 
         each(1, D, send_block)
@@ -395,17 +398,16 @@
     pose, back = pl.pallas_call(
         body,
         out_shape=(jax.ShapeDtypeStruct((1, PART), F32), jax.ShapeDtypeStruct((3, R, X), F32)),
-        in_specs=[hbm] * 5,
+        in_specs=[hbm] * 4,
         out_specs=(vmem, vmem),
         scratch_shapes=[
             pltpu.VMEM((SLAB, R, X), F32),
             pltpu.VMEM((PART, R, U), BF16),
             pltpu.VMEM((NCTF, 2, U), F32),
             pltpu.SMEM((PART,), jnp.int32),
-            pltpu.SMEM((PART,), jnp.int32),
             pltpu.SMEM((NU,), jnp.int32),
             pltpu.SMEM((NU,), jnp.int32),
-            dma((5,)),
+            dma((4,)),
             pltpu.VMEM((2 * R * SLAB, X), BF16),
             pltpu.VMEM((NB_DEV, X, 2 * U), BF16),
             pltpu.VMEM((NB_DEV, SLAB, U), F32),
@@ -435,9 +437,9 @@
             dma((BLOCKS,)), dma((BLOCKS,)), dma, dma,
         ],
         compiler_params=pltpu.CompilerParams(
-            collective_id=0, has_side_effects=True, vmem_limit_bytes=60 << 20),
+            collective_id=0, has_side_effects=True, vmem_limit_bytes=55200 << 10),
         name="tilt_refine",
-    )(volume, observed, ctf_table, ctf_class, bin_ids)
+    )(volume, observed, ctf_table, NCTF * bin_ids + ctf_class)
     return (pose.reshape(PART), back)
 
 

time: 45.8 us -> 43.2 us (0.943)
  Pallas kernels: 42.6 us -> 40.7 us
  local copies, waits for them, and re-layouts: 2.47 us -> 1.12 us
  other arithmetic: 0 us -> 0.68 us
    pallas_call x1, Pallas kernels: 42.6 us -> 40.7 us  [local(): pl.pallas_call(body, out_shape=(jax.ShapeDtypeStruct((1, PART), F32), jax...]
    unnamed x4 -> x2, local copies, waits for them, and re-layouts: 2.47 us -> 1.12 us
    add x0 -> x1, other arithmetic: none -> 0.68 us  [local(): NCTF * bin_ids + ctf_class]
where the time goes in v8:
time: 43.2 us; the launch traced here: 43.1 us
  Pallas kernels  40.7 us (94%)
  local copies, waits for them, and re-layouts  1.12 us (3%)
  other arithmetic  0.68 us (2%)
  between operations  0.64 us (1%)
    pallas_call x1, Pallas kernels, local(): pl.pallas_call(body, out_shape=(jax.ShapeDtypeStruct((1, PART), F32), jax...  40.7 us
    unnamed x2, local copies, waits for them, and re-layouts  1.12 us

profile of v8, /device:TPU:1, one launch (start us, length us, event | category | flops | bytes accessed | tf_op | source)
XLA Modules:
  0.0 43.1 jit_solution(15226381850306632833)
XLA Ops:
  0.6 0.7 %multiply_add_fusion.mark_hbm = s32[16]{0:T(128)S(1)} fusion(s32[16]{0:T(128)} %param.8, s32[16]{0:T(128)} %param.9), kind=kLoop, calls=%fused_computation | loop fusion | flops 32 | bytes 192 | tf_op jit(solution)/shard_map/add | solution.py:442
  1.3 40.7 %tilt_refine.1 = (f32[1,16]{1,0:T(1,128)S(1)}, f32[3,4,384]{2,1,0:T(4,128)S(1)}) custom-call(f32[48,4,384]{2,1,0:T(4,128)} %vol_hbm.1, bf16[16,4,384]{2,1,0:T(4,128)(2,1)} %obs_hbm.1, f32[32,2,384]{2,1,0:T(2,128)} %ctf_hbm.1, s32[16]{0:T(128)S(1)} %multiply_add_fusion.mark_hbm), custom_call_target="tpu_custom_call" | custom-call | tf_op jit(solution)/shard_map/tilt_refine/pallas_call | solution.py:398
  42.0 0.5 %copy.9 = f32[16]{0:T(128)} copy(f32[16]{0:T(128)S(1)} %bitcast.1) | data formatting | bytes 128
  42.5 0.6 %copy.10 = f32[3,4,384]{2,1,0:T(4,128)} copy(f32[3,4,384]{2,1,0:T(4,128)S(1)} %get-tuple-element.9) | data formatting | bytes 36864

commit v9 on v8

--- a/solution.py
+++ b/solution.py
@@ -134,8 +134,14 @@
 
     pl.semaphore_wait(barrier, (G - 1) + (D - 1))
 
-    each(1, D // 2, lambda i: dom_copy(
-        w_all.at[d], w_all.at[d], w_send, w_recv.at[d], lax.rem(zpos + far_first(i, D // 2), D // 2) * 2 + core).start())
+    def device_at(step, on):
+        return lax.rem(zpos + step, D // 2) * 2 + on
+
+    def step_of(i):
+        return D // 4 + lax.div(i + 1, 2) * (2 * lax.rem(i, 2) - 1)
+
+    each(1, D // 2 - 1, lambda i: dom_copy(
+        w_all.at[d], w_all.at[d], w_send, w_recv.at[d], device_at(step_of(i), core)).start())
     dom_copy(w_all.at[d], w_all.at[d], f_send, f_recv, sib).start()
     each(1, D, lambda i: dom_copy(ids, ids_in.at[d], i_send, i_recv, lax.rem(d + i, D)).start())
 
@@ -212,12 +218,18 @@
 
     each(0, NU, send_slices)
 
-    def pass_on(i):
-        frm = lax.rem(zpos + far_first(i, D // 2), D // 2) * 2 + core
-        dom_copy(w_all.at[frm], w_all.at[frm], w_recv.at[frm], w_recv.at[frm], sib).wait_recv()
-        dom_copy(w_all.at[frm], w_all.at[frm], f_send, f_recv, sib).start()
-
-    each(1, D // 2, pass_on)
+    def pass_on(i, relay=None):
+        frm = device_at(step_of(i), core)
+        block = w_all.at[frm]
+        dom_copy(block, block, w_recv.at[frm], w_recv.at[frm], sib).wait_recv()
+        if relay is not None:
+            dom_copy(block, block, w_send, w_recv.at[frm], relay).start()
+        dom_copy(block, block, f_send, f_recv, sib).start()
+
+    pass_on(jnp.int32(1), device_at(1, core))
+    pass_on(jnp.int32(2), device_at(D // 2 - 1, 1 - core))
+    each(3, D // 2 - 1, pass_on)
+
     def gather_slices(n):
         def gather(frm, total):
             @pl.when(frm != g)
@@ -273,8 +285,12 @@
     sloped_row = lax.rem(lax.div(slot, 2), 2) == 1
     mask_rows = (2 * d + 2 * D * lax.div(slot, 4) + lax.rem(slot, 2) == bin_row).astype(F32)
 
-    half = w_all.at[0:D // 2]
-    dom_copy(half, half, f_recv, f_recv, sib).wait_recv()
+    for on in (core, 1 - core):
+        frm = device_at(D // 4, on)
+        block = w_all.at[frm]
+        dom_copy(block, block, w_recv.at[frm], w_recv.at[frm], sib).wait_recv()
+    passed = w_all.at[0:D // 2 - 1]
+    dom_copy(passed, passed, f_recv, f_recv, sib).wait_recv()
 
     images = w_all[...].reshape(ALLP, WC)
     along = lax.dot_general(slope_rows, images, NT, preferred_element_type=F32)
@@ -370,9 +386,9 @@
         each_slab(n, lambda copy: copy.wait_send())
 
     each(0, NU, finish)
-    sent = w_all.at[0:D // 2 - 1]
+    sent = w_all.at[0:D // 2]
     dom_copy(sent, sent, w_send, w_send, sib).wait_send()
-    dom_copy(half, half, f_send, f_send, sib).wait_send()
+    dom_copy(passed, passed, f_send, f_send, sib).wait_send()
     sent = pose_in.at[0:D - 1]
     dom_copy(sent, sent, p_send, p_send, sib).wait_send()
     sent = ids_in.at[0:D - 1]

time: 43.2 us -> 40.8 us (0.944)
  Pallas kernels: 40.7 us -> 38.3 us
    pallas_call x1, Pallas kernels: 40.7 us -> 38.3 us  [local(): pl.pallas_call(body, out_shape=(jax.ShapeDtypeStruct((1, PART), F32), jax...]
where the time goes in v9:
time: 40.8 us; the launch traced here: 40.7 us
  Pallas kernels  38.3 us (94%)
  local copies, waits for them, and re-layouts  1.12 us (3%)
  other arithmetic  0.68 us (2%)
  between operations  0.64 us (2%)
    pallas_call x1, Pallas kernels, local(): pl.pallas_call(body, out_shape=(jax.ShapeDtypeStruct((1, PART), F32), jax...  38.3 us
    unnamed x2, local copies, waits for them, and re-layouts  1.12 us

profile of v9, /device:TPU:1, one launch (start us, length us, event | category | flops | bytes accessed | tf_op | source)
XLA Modules:
  0.0 40.7 jit_solution(11458808915603611072)
XLA Ops:
  0.6 0.7 %multiply_add_fusion.mark_hbm = s32[16]{0:T(128)S(1)} fusion(s32[16]{0:T(128)} %param.8, s32[16]{0:T(128)} %param.9), kind=kLoop, calls=%fused_computation | loop fusion | flops 32 | bytes 192 | tf_op jit(solution)/shard_map/add | solution.py:458
  1.3 38.3 %tilt_refine.1 = (f32[1,16]{1,0:T(1,128)S(1)}, f32[3,4,384]{2,1,0:T(4,128)S(1)}) custom-call(f32[48,4,384]{2,1,0:T(4,128)} %vol_hbm.1, bf16[16,4,384]{2,1,0:T(4,128)(2,1)} %obs_hbm.1, f32[32,2,384]{2,1,0:T(2,128)} %ctf_hbm.1, s32[16]{0:T(128)S(1)} %multiply_add_fusion.mark_hbm), custom_call_target="tpu_custom_call" | custom-call | tf_op jit(solution)/shard_map/tilt_refine/pallas_call | solution.py:414
  39.6 0.5 %copy.9 = f32[16]{0:T(128)} copy(f32[16]{0:T(128)S(1)} %bitcast.1) | data formatting | bytes 128
  40.1 0.6 %copy.10 = f32[3,4,384]{2,1,0:T(4,128)} copy(f32[3,4,384]{2,1,0:T(4,128)S(1)} %get-tuple-element.9) | data formatting | bytes 36864

commit v10 on v9

--- a/solution.py
+++ b/solution.py
@@ -93,7 +93,7 @@
 
     barrier = pltpu.get_barrier_semaphore()
     each(1, D, lambda i: pl.semaphore_signal(
-        barrier, inc=1, device_id={"dom": lax.rem(d + i, D)}, device_id_type=pl.DeviceIdType.MESH))
+        barrier, inc=1, device_id={"dom": lax.rem(d + far_first(i, D), D)}, device_id_type=pl.DeviceIdType.MESH))
     each(1, G, lambda i: pl.semaphore_signal(
         barrier, inc=1, device_id={"gz": lax.rem(g + i, G)}, device_id_type=pl.DeviceIdType.MESH))
 
@@ -167,7 +167,7 @@
     sc[:NB_DEV, :] = jnp.sin(theta)
     sc[NB_DEV:, :] = jnp.cos(theta)
 
-    for j in range(BLOCKS):
+    for j in reversed(range(BLOCKS)):
         wide = BL * (j + 1)
         radius = (BL * j + iota((1, BL), 1)).astype(F32)
         plane = (g * SLAB + iota((SLAB, BL), 0)).astype(F32)
@@ -203,20 +203,16 @@
             spb[n] = sp[n].astype(BF16)
 
         def unit(k, j=j, extract=extract):
-            @pl.when(active(PAIRS * j + k, g))
+            n = PAIRS * j + k
+
+            @pl.when(active(n, g))
             def _():
-                extract(PAIRS * j + k, k)
+                extract(n, k)
+                each(1, G, lambda i: gz_copy(
+                    spb.at[n], sp_in.at[n, g], rs_send.at[n], rs_recv.at[n, g], lax.rem(g + i, G)).start())
+                sp_in[n, g] = spb[n]
 
         each(0, PAIRS, unit)
-
-    def send_slices(n):
-        @pl.when(active(n, g))
-        def _():
-            each(1, G, lambda i: gz_copy(
-                spb.at[n], sp_in.at[n, g], rs_send.at[n], rs_recv.at[n, g], lax.rem(g + i, G)).start())
-            sp_in[n, g] = spb[n]
-
-    each(0, NU, send_slices)
 
     def pass_on(i, relay=None):
         frm = device_at(step_of(i), core)
@@ -363,7 +359,7 @@
         bk[j] = ordered.astype(BF16).reshape(D, 16, BL)
         def send_block(i, j=j):
             to = lax.rem(d + far_first(i, D), D)
-            dom_copy(bk.at[j, to], bk_in.at[j, d], b_send.at[j], b_recv.at[j], to).start()
+            dom_copy(bk.at[j, to, 0:12], bk_in.at[j, d, 0:12], b_send.at[j], b_recv.at[j], to).start()
 
         each(1, D, send_block)
 
@@ -396,14 +392,14 @@
 
     for j in reversed(range(BLOCKS)):
         bk_in[j, d] = bk[j, d]
-        others = bk_in.at[j, 0:D - 1]
+        others = bk_in.at[j, 0:D - 1, 0:12]
         dom_copy(others, others, b_recv.at[j], b_recv.at[j], sib).wait_recv()
         total = jnp.sum(bk_in[j].astype(F32), axis=0)
         for k in range(3):
             back_out[k, :, BL * j:BL * (j + 1)] = total[4 * k:4 * k + 4]
 
     for j in range(BLOCKS):
-        sent = bk_in.at[j, 0:D - 1]
+        sent = bk_in.at[j, 0:D - 1, 0:12]
         dom_copy(sent, sent, b_send.at[j], b_send.at[j], sib).wait_send()
 
 

time: 40.8 us -> 40.1 us (0.983)
  Pallas kernels: 38.3 us -> 37.5 us
    pallas_call x1, Pallas kernels: 38.3 us -> 37.5 us  [local(): pl.pallas_call(body, out_shape=(jax.ShapeDtypeStruct((1, PART), F32), jax...]
where the time goes in v10:
time: 40.1 us; the launch traced here: 40 us
  Pallas kernels  37.5 us (94%)
  local copies, waits for them, and re-layouts  1.12 us (3%)
  other arithmetic  0.68 us (2%)
  between operations  0.64 us (2%)
    pallas_call x1, Pallas kernels, local(): pl.pallas_call(body, out_shape=(jax.ShapeDtypeStruct((1, PART), F32), jax...  37.5 us
    unnamed x2, local copies, waits for them, and re-layouts  1.12 us

profile of v10, /device:TPU:1, one launch (start us, length us, event | category | flops | bytes accessed | tf_op | source)
XLA Modules:
  0.0 40.0 jit_solution(5302545570616334561)
XLA Ops:
  0.6 0.7 %multiply_add_fusion.mark_hbm = s32[16]{0:T(128)S(1)} fusion(s32[16]{0:T(128)} %param.8, s32[16]{0:T(128)} %param.9), kind=kLoop, calls=%fused_computation | loop fusion | flops 32 | bytes 192 | tf_op jit(solution)/shard_map/add | solution.py:454
  1.3 37.5 %tilt_refine.1 = (f32[1,16]{1,0:T(1,128)S(1)}, f32[3,4,384]{2,1,0:T(4,128)S(1)}) custom-call(f32[48,4,384]{2,1,0:T(4,128)} %vol_hbm.1, bf16[16,4,384]{2,1,0:T(4,128)(2,1)} %obs_hbm.1, f32[32,2,384]{2,1,0:T(2,128)} %ctf_hbm.1, s32[16]{0:T(128)S(1)} %multiply_add_fusion.mark_hbm), custom_call_target="tpu_custom_call" | custom-call | tf_op jit(solution)/shard_map/tilt_refine/pallas_call | solution.py:410
  38.9 0.5 %copy.9 = f32[16]{0:T(128)} copy(f32[16]{0:T(128)S(1)} %bitcast.1) | data formatting | bytes 128
  39.4 0.6 %copy.10 = f32[3,4,384]{2,1,0:T(4,128)} copy(f32[3,4,384]{2,1,0:T(4,128)S(1)} %get-tuple-element.9) | data formatting | bytes 36864

commit v11 on v10

--- a/solution.py
+++ b/solution.py
@@ -64,12 +64,12 @@
         device_id={"dom": to}, device_id_type=pl.DeviceIdType.MESH)
 
 
-def each(first, last, act):
+def each(first, last, act, unroll=1):
     def one(i, carry):
         act(i)
         return carry
 
-    lax.fori_loop(first, last, one, 0)
+    lax.fori_loop(first, last, one, 0, unroll=unroll)
 
 
 def far_first(i, n):
@@ -138,9 +138,9 @@
         return lax.rem(zpos + step, D // 2) * 2 + on
 
     def step_of(i):
-        return D // 4 + lax.div(i + 1, 2) * (2 * lax.rem(i, 2) - 1)
-
-    each(1, D // 2 - 1, lambda i: dom_copy(
+        return D // 4 + (1 + lax.div(i + 1, 2)) * (2 * lax.rem(i, 2) - 1)
+
+    each(1, 5, lambda i: dom_copy(
         w_all.at[d], w_all.at[d], w_send, w_recv.at[d], device_at(step_of(i), core)).start())
     dom_copy(w_all.at[d], w_all.at[d], f_send, f_recv, sib).start()
     each(1, D, lambda i: dom_copy(ids, ids_in.at[d], i_send, i_recv, lax.rem(d + i, D)).start())
@@ -214,17 +214,19 @@
 
         each(0, PAIRS, unit)
 
-    def pass_on(i, relay=None):
-        frm = device_at(step_of(i), core)
+    def pass_on(step, relays=()):
+        frm = device_at(step, core)
         block = w_all.at[frm]
         dom_copy(block, block, w_recv.at[frm], w_recv.at[frm], sib).wait_recv()
-        if relay is not None:
+        for relay in relays:
             dom_copy(block, block, w_send, w_recv.at[frm], relay).start()
         dom_copy(block, block, f_send, f_recv, sib).start()
 
-    pass_on(jnp.int32(1), device_at(1, core))
-    pass_on(jnp.int32(2), device_at(D // 2 - 1, 1 - core))
-    each(3, D // 2 - 1, pass_on)
+    pass_on(6, (device_at(2, core), device_at(1, core)))
+    pass_on(2, (device_at(6, 1 - core), device_at(7, core)))
+    each(3, 5, lambda i: pass_on(step_of(i)))
+    pass_on(5)
+    pass_on(3)
 
     def gather_slices(n):
         def gather(frm, total):
@@ -361,7 +363,7 @@
             to = lax.rem(d + far_first(i, D), D)
             dom_copy(bk.at[j, to, 0:12], bk_in.at[j, d, 0:12], b_send.at[j], b_recv.at[j], to).start()
 
-        each(1, D, send_block)
+        each(1, D, send_block, 15)
 
     pose_in[d] = pose_s[...]
     others = pose_in.at[0:D - 1]

time: 40.1 us -> 39.8 us (level)
  no operation moved by 1% of the time
where the time goes in v11:
time: 39.8 us; the launch traced here: 39.7 us
  Pallas kernels  37.3 us (94%)
  local copies, waits for them, and re-layouts  1.12 us (3%)
  other arithmetic  0.68 us (2%)
  between operations  0.64 us (2%)
    pallas_call x1, Pallas kernels, local(): pl.pallas_call(body, out_shape=(jax.ShapeDtypeStruct((1, PART), F32), jax...  37.3 us
    unnamed x2, local copies, waits for them, and re-layouts  1.12 us

profile of v11, /device:TPU:1, one launch (start us, length us, event | category | flops | bytes accessed | tf_op | source)
XLA Modules:
  0.0 39.7 jit_solution(5716644006132227718)
XLA Ops:
  0.6 0.7 %multiply_add_fusion.mark_hbm = s32[16]{0:T(128)S(1)} fusion(s32[16]{0:T(128)} %param.8, s32[16]{0:T(128)} %param.9), kind=kLoop, calls=%fused_computation | loop fusion | flops 32 | bytes 192 | tf_op jit(solution)/shard_map/add | solution.py:456
  1.3 37.3 %tilt_refine.1 = (f32[1,16]{1,0:T(1,128)S(1)}, f32[3,4,384]{2,1,0:T(4,128)S(1)}) custom-call(f32[48,4,384]{2,1,0:T(4,128)} %vol_hbm.1, bf16[16,4,384]{2,1,0:T(4,128)(2,1)} %obs_hbm.1, f32[32,2,384]{2,1,0:T(2,128)} %ctf_hbm.1, s32[16]{0:T(128)S(1)} %multiply_add_fusion.mark_hbm), custom_call_target="tpu_custom_call" | custom-call | tf_op jit(solution)/shard_map/tilt_refine/pallas_call | solution.py:412
  38.6 0.5 %copy.9 = f32[16]{0:T(128)} copy(f32[16]{0:T(128)S(1)} %bitcast.1) | data formatting | bytes 128
  39.1 0.6 %copy.10 = f32[3,4,384]{2,1,0:T(4,128)} copy(f32[3,4,384]{2,1,0:T(4,128)S(1)} %get-tuple-element.9) | data formatting | bytes 36864

commit v12 on v11

--- a/solution.py
+++ b/solution.py
@@ -77,7 +77,7 @@
 
 
 def body(vol_hbm, obs_hbm, ctf_hbm, mark_hbm, pose_out, back_out,
-         vol, obs, ctf, mark, low, top, in_sem, vb, kt, kz, kzd, sc, sp, spb, sp_in, s_all, sf, ss, ss_in, rows_t,
+         vol, obs, ctf, mark, low, top, in_sem, vb, kt, kl, kz, kzd, sc, sp, spb, sp_in, s_all, sf, ss, ss_in, rows_t,
          w_all, c2h, c2l, acc, bk, bk_in, pose_s, pose_in,
          ids, ids_in, w_send, w_recv, f_send, f_recv, i_send, i_recv,
          rs_send, rs_recv, rs2_send, rs2_recv, b_send, b_recv, p_send, p_recv):
@@ -184,6 +184,7 @@
                 kx_high = kx.astype(BF16)
                 kt[b, :wide, 2 * BL * j:2 * BL * (j + 1)] = kx_high
                 kx_low = (kx - kx_high.astype(F32)).astype(BF16)
+                kl[b, :wide, 2 * BL * j:2 * BL * (j + 1)] = kx_low
                 tz = plane - (0.5 * NZ + radius * sine)
                 fz = jnp.maximum(1.0 - tz * tz, 0.0)
                 wz = fz * fz
@@ -348,7 +349,8 @@
                 both = lax.dot_general(
                     jnp.concatenate([left_high, left_low], 0),
                     kt[b, :wide, 2 * BL * j:2 * BL * (j + 1)], NT, preferred_element_type=F32)
-                acc[:, :wide] += both[:R * SLAB] + both[R * SLAB:]
+                acc[:, :wide] += both[:R * SLAB] + both[R * SLAB:] + lax.dot_general(
+                    left_high, kl[b, :wide, 2 * BL * j:2 * BL * (j + 1)], NT, preferred_element_type=F32)
 
         def unit(k, j=j, spread_back=spread_back):
             @pl.when(active(PAIRS * j + k, g))
@@ -423,6 +425,7 @@
             pltpu.SMEM((NU,), jnp.int32),
             dma((4,)),
             pltpu.VMEM((2 * R * SLAB, X), BF16),
+            pltpu.VMEM((NB_DEV, X, 2 * U), BF16),
             pltpu.VMEM((NB_DEV, X, 2 * U), BF16),
             pltpu.VMEM((NB_DEV, SLAB, U), F32),
             pltpu.VMEM((NB_DEV, SLAB, U), F32),

time: 39.8 us -> 39.9 us (level)
  no operation moved by 1% of the time
where the time goes in v12:
time: 39.9 us; the launch traced here: 39.8 us
  Pallas kernels  37.4 us (94%)
  local copies, waits for them, and re-layouts  1.12 us (3%)
  other arithmetic  0.68 us (2%)
  between operations  0.64 us (2%)
    pallas_call x1, Pallas kernels, local(): pl.pallas_call(body, out_shape=(jax.ShapeDtypeStruct((1, PART), F32), jax...  37.4 us
    unnamed x2, local copies, waits for them, and re-layouts  1.12 us

profile of v12, /device:TPU:1, one launch (start us, length us, event | category | flops | bytes accessed | tf_op | source)
XLA Modules:
  0.0 39.8 jit_solution(17163067791327753668)
XLA Ops:
  0.6 0.7 %multiply_add_fusion.mark_hbm = s32[16]{0:T(128)S(1)} fusion(s32[16]{0:T(128)} %param.8, s32[16]{0:T(128)} %param.9), kind=kLoop, calls=%fused_computation | loop fusion | flops 32 | bytes 192 | tf_op jit(solution)/shard_map/add | solution.py:459
  1.3 37.4 %tilt_refine.1 = (f32[1,16]{1,0:T(1,128)S(1)}, f32[3,4,384]{2,1,0:T(4,128)S(1)}) custom-call(f32[48,4,384]{2,1,0:T(4,128)} %vol_hbm.1, bf16[16,4,384]{2,1,0:T(4,128)(2,1)} %obs_hbm.1, f32[32,2,384]{2,1,0:T(2,128)} %ctf_hbm.1, s32[16]{0:T(128)S(1)} %multiply_add_fusion.mark_hbm), custom_call_target="tpu_custom_call" | custom-call | tf_op jit(solution)/shard_map/tilt_refine/pallas_call | solution.py:414
  38.7 0.5 %copy.9 = f32[16]{0:T(128)} copy(f32[16]{0:T(128)S(1)} %bitcast.1) | data formatting | bytes 128
  39.2 0.6 %copy.10 = f32[3,4,384]{2,1,0:T(4,128)} copy(f32[3,4,384]{2,1,0:T(4,128)S(1)} %get-tuple-element.9) | data formatting | bytes 36864

commit v13 on v12

--- a/solution.py
+++ b/solution.py
@@ -226,9 +226,6 @@
     pass_on(6, (device_at(2, core), device_at(1, core)))
     pass_on(2, (device_at(6, 1 - core), device_at(7, core)))
     each(3, 5, lambda i: pass_on(step_of(i)))
-    pass_on(5)
-    pass_on(3)
-
     def gather_slices(n):
         def gather(frm, total):
             @pl.when(frm != g)
@@ -284,6 +281,8 @@
     sloped_row = lax.rem(lax.div(slot, 2), 2) == 1
     mask_rows = (2 * d + 2 * D * lax.div(slot, 4) + lax.rem(slot, 2) == bin_row).astype(F32)
 
+    pass_on(5)
+    pass_on(3)
     for on in (core, 1 - core):
         frm = device_at(D // 4, on)
         block = w_all.at[frm]

time: 39.9 us -> 39.8 us (level)
  no operation moved by 1% of the time
where the time goes in v13:
time: 39.8 us; the launch traced here: 39.6 us
  Pallas kernels  37.2 us (93%)
  local copies, waits for them, and re-layouts  1.12 us (3%)
  other arithmetic  0.68 us (2%)
  between operations  0.64 us (2%)
    pallas_call x1, Pallas kernels, local(): pl.pallas_call(body, out_shape=(jax.ShapeDtypeStruct((1, PART), F32), jax...  37.2 us
    unnamed x2, local copies, waits for them, and re-layouts  1.12 us

profile of v13, /device:TPU:1, one launch (start us, length us, event | category | flops | bytes accessed | tf_op | source)
XLA Modules:
  0.0 39.6 jit_solution(11654876625713909506)
XLA Ops:
  0.6 0.7 %multiply_add_fusion.mark_hbm = s32[16]{0:T(128)S(1)} fusion(s32[16]{0:T(128)} %param.8, s32[16]{0:T(128)} %param.9), kind=kLoop, calls=%fused_computation | loop fusion | flops 32 | bytes 192 | tf_op jit(solution)/shard_map/add | solution.py:458
  1.3 37.2 %tilt_refine.1 = (f32[1,16]{1,0:T(1,128)S(1)}, f32[3,4,384]{2,1,0:T(4,128)S(1)}) custom-call(f32[48,4,384]{2,1,0:T(4,128)} %vol_hbm.1, bf16[16,4,384]{2,1,0:T(4,128)(2,1)} %obs_hbm.1, f32[32,2,384]{2,1,0:T(2,128)} %ctf_hbm.1, s32[16]{0:T(128)S(1)} %multiply_add_fusion.mark_hbm), custom_call_target="tpu_custom_call" | custom-call | tf_op jit(solution)/shard_map/tilt_refine/pallas_call | solution.py:413
  38.5 0.5 %copy.9 = f32[16]{0:T(128)} copy(f32[16]{0:T(128)S(1)} %bitcast.1) | data formatting | bytes 128
  39.0 0.6 %copy.10 = f32[3,4,384]{2,1,0:T(4,128)} copy(f32[3,4,384]{2,1,0:T(4,128)S(1)} %get-tuple-element.9) | data formatting | bytes 36864
